TPU v7x, 256 devices: a whole 4x4x8 slice. The times are simulated.
256 devices in a mesh: unit: 16 (over x, z_lo), day: 16 (over y, z_hi, core).
Axes of the slice: x: 4, y: 4, z: 8 (z_hi: 2, z_lo: 4; z = z_hi * 4 + z_lo), core: 2. Of those that a mesh axis runs over, the one named last changes fastest.
Arguments:
- outcomes: float32 [65536, 4096], P('unit', 'day'), may hold values from -6 to 6
- cohort: int32 [65536], P('unit'), may hold values from 0 to 8
- pre_end: int32 [8], replicated, may hold values from 1024 to 2047
- post_start: int32 [8], replicated, may hold values from 2048 to 3071
- unit_logit: float32 [8, 65536], P(None, 'unit'), may hold values from -4 to 4
- time_logit: float32 [8, 4096], P(None, 'day'), may hold values from -4 to 4
Outputs:
- unit_weights: float32 [8, 65536], P(None, 'unit')
- time_weights: float32 [8, 4096], P(None, 'day')
All inputs are finite; a program needn't handle non-finite values.
Results may differ from a plain program's by a relative error of at most 0.0003.
Values sent between devices are 32-bit elements; how exact they have to be, the bound alone decides.
A program may use at most 64 MiB of HBM per device.

v0:
```python
import jax
import jax.numpy as jnp
from jax import lax
from jax.sharding import PartitionSpec as P

highest = lax.Precision.HIGHEST
step_rate = 16.0


def weigh_rows(left, outcomes):
    return jnp.dot(left, outcomes, precision=highest, preferred_element_type=jnp.float32)


def weigh_days(left, outcomes):
    return lax.dot_general(
        left,
        outcomes,
        (((1,), (1,)), ((), ())),
        precision=highest,
        preferred_element_type=jnp.float32,
    )


def local(outcomes, cohort, pre_end, post_start, unit_logit, time_logit):
    groups = pre_end.shape[0]
    unit_rows, day_cols = outcomes.shape
    day_devices = lax.axis_size("day")
    all_count = day_devices * day_cols
    labels = jnp.arange(groups, dtype=jnp.int32)[:, None]
    treated = (cohort[None, :] == labels).astype(jnp.float32)
    control = (cohort[None, :] > labels).astype(jnp.float32)
    day_start = lax.axis_index("day") * day_cols
    day_index = day_start + jnp.arange(day_cols, dtype=jnp.int32)[None, :]
    before = (day_index < pre_end[:, None]).astype(jnp.float32)
    before_len = pre_end.astype(jnp.float32)
    after_len = (all_count - post_start).astype(jnp.float32)
    raised = jnp.exp(unit_logit) * control
    unit_norm, treat_count, ctrl_count = lax.psum(
        (jnp.sum(raised, axis=1), jnp.sum(treated, axis=1), jnp.sum(control, axis=1)), "unit"
    )
    weights = raised / unit_norm[:, None]
    fitted, treat_sum = lax.psum(
        (weigh_rows(weights, outcomes), weigh_rows(treated, outcomes)), "unit"
    )
    residual = (fitted - treat_sum / jnp.maximum(treat_count, 1.0)[:, None]) * before
    ctrl_root = jnp.sqrt(jnp.maximum(ctrl_count, 1.0))[:, None]
    relaid = lax.all_to_all(outcomes, "day", split_axis=0, concat_axis=1, tiled=True)
    slab_rows = unit_rows // day_devices
    full_resid, full_logit = (
        lax.all_gather(residual, "day", axis=1, tiled=True),
        lax.all_gather(time_logit, "day", axis=1, tiled=True),
    )
    all_days = jnp.arange(all_count, dtype=jnp.int32)[None, :]
    full_before = (all_days < pre_end[:, None]).astype(jnp.float32)
    full_after = (all_days >= post_start[:, None]).astype(jnp.float32)
    row_start = lax.axis_index("day") * slab_rows
    sub_control = lax.dynamic_slice_in_dim(control, row_start, slab_rows, 1)
    sub_weights = lax.dynamic_slice_in_dim(weights, row_start, slab_rows, 1)
    unit_grad = weigh_days(full_resid, relaid)
    updated = sub_weights * jnp.exp(-step_rate * unit_grad / jnp.sqrt(before_len)[:, None])
    unit_total = lax.psum(jnp.sum(updated, axis=1), ("unit", "day"))
    row_share = updated / unit_total[:, None] * ctrl_count[:, None]
    unit_weights = lax.all_gather(row_share, "day", axis=1, tiled=True)
    time_raised = jnp.exp(full_logit) * full_before
    time_lam = time_raised / jnp.sum(time_raised, axis=1)[:, None]
    time_fit = weigh_days(time_lam, relaid)
    post_sum = weigh_days(full_after, relaid)
    shortfall = (time_fit - post_sum / after_len[:, None]) * sub_control
    time_grad = lax.psum(weigh_rows(shortfall, relaid), ("unit", "day"))
    moved = time_lam * jnp.exp(-step_rate * time_grad / ctrl_root)
    full_weights = moved / jnp.sum(moved, axis=1)[:, None] * before_len[:, None]
    time_weights = lax.dynamic_slice_in_dim(full_weights, day_start, day_cols, 1)
    return (unit_weights, time_weights)


def solution(mesh):
    return jax.shard_map(
        local,
        mesh=mesh,
        in_specs=(P("unit", "day"), P("unit"), P(), P(), P(None, "unit"), P(None, "day")),
        out_specs=(P(None, "unit"), P(None, "day")),
        check_vma=False,
    )
```

profile of v0, /device:TPU:1, one launch (start us, length us, event | category | flops | bytes accessed | tf_op | source)
XLA Modules:
  0.0 548.6 jit_solution(5261238960471951254)
XLA Ops:
  7.2 0.0 copy-start.2
  7.2 0.0 copy-start.3
  7.2 0.0 copy-start.4
  7.2 12.7 %all-to-all-start = ((f32[16,256,256]{2,1,0:T(8,128)}), f32[16,256,256]{2,1,0:T(8,128)}, u32[]{:S(2)}, u32[]{:S(2)}) async-start(f32[16,256,256]{2,1,0:T(8,128)} %bitcast.16), calls=%async_computation | async-start | bytes 8388608 | tf_op jit(solution)/shard_map/all_to_all | solution.py:47
  19.9 0.0 all-reduce.3.cloned.1.call-start
  20.0 0.0 copy-done.2
  20.0 0.0 copy-done.3
  20.0 0.2 fusion.13
  20.2 122.6 %psum.49 = f32[8]{0:T(128)S(1)} all-reduce(f32[8]{0:T(128)S(1)} %get-tuple-element.4), channel_id=1, replica_groups=mesh['unit'=16,'day'=16] {'unit'}, use_global_device_ids=true, to_apply=%region_1.0 | all-reduce | flops 8 | bytes 64 | tf_op jit(solution)/shard_map/psum | solution.py:38
  142.8 0.0 copy-done.4
  142.8 0.0 copy-start.1
  142.8 0.0 copy-start.5
  142.8 0.0 copy-start.6
  142.8 3.8 fusion.5
  146.6 0.1 fusion.7
  146.7 0.0 copy-done.1
  146.7 1.7 fusion.19
  148.5 60.7 %all-reduce = (f32[8,256]{1,0:T(8,128)S(1)}, f32[8,256]{1,0:T(8,128)S(1)}, f32[8]{0:T(128)S(1)}, f32[8]{0:T(128)S(1)}) all-reduce(f32[8,256]{1,0:T(8,128)S(1)} %fusion.19, f32[8,256]{1,0:T(8,128)S(1)} %fusion.5, f32[8]{0:T(128)S(1)} %get-tuple-element.3, f32[8]{0:T(128)S(1)} %get-tuple-element.2), channel_id=1, replica_groups=mesh['unit'=16,'day'=16] {'unit'}, use_global_device_ids=true, to_apply=%region_2.0 | all-reduce | flops 4112 | bytes 32896 | tf_op jit(solution)/shard_map/psum | solution.py:42
  209.1 0.0 copy-done.5
  209.1 49.2 %all_gather.11 = f32[8,4096]{1,0:T(8,128)S(1)} all-gather(f32[8,256]{1,0:T(8,128)S(1)} %copy-done.5), channel_id=1, replica_groups=mesh['unit'=16,'day'=16] {'day'}, dimensions={1}, use_global_device_ids=true | all-gather | bytes 139264 | tf_op jit(solution)/shard_map/all_gather | solution.py:51
  258.3 0.1 subtract_select_fusion
  258.4 25.8 %all_gather.9 = f32[8,4096]{1,0:T(8,128)S(1)} all-gather(f32[8,256]{1,0:T(8,128)S(1)} %subtract_select_fusion), channel_id=1, replica_groups=mesh['unit'=16,'day'=16] {'day'}, dimensions={1}, use_global_device_ids=true | all-gather | bytes 139264 | tf_op jit(solution)/shard_map/all_gather | solution.py:50
  284.2 0.2 fusion.10
  284.4 0.0 copy-done.6
  284.5 0.0 all-to-all-done
  284.5 5.4 copy.8
  289.9 0.0 copy-start
  289.9 4.2 fusion.15
  294.0 0.0 copy-done
  294.0 1.5 fusion.1
  295.5 4.2 fusion.20
  299.7 0.0 all-reduce.3.cloned.1.call-update
  299.7 4.0 fusion.18
  303.8 73.0 %psum.53 = f32[8]{0:T(128)S(1)} all-reduce(f32[8]{0:T(128)S(1)} %get-tuple-element.11), channel_id=1, replica_groups=mesh['unit'=16,'day'=16] {'unit','day'}, use_global_device_ids=true, to_apply=%region_7.0 | all-reduce | flops 8 | bytes 64 | tf_op jit(solution)/shard_map/psum | solution.py:61
  376.7 0.1 divide_multiply_fusion
  376.8 30.0 %all_gather.10 = f32[8,4096]{1,0:T(8,128)S(1)} all-gather(f32[8,256]{1,0:T(8,128)S(1)} %divide_multiply_fusion), channel_id=1, replica_groups=mesh['unit'=16,'day'=16] {'day'}, dimensions={1}, use_global_device_ids=true | all-gather | bytes 139264 | tf_op jit(solution)/shard_map/all_gather | solution.py:63
  406.8 132.5 %all-reduce.3.cloned.1.call-done = f32[8,4096]{1,0:T(8,128)} async-done(((f32[8,4096]{1,0:T(8,128)}), f32[8,4096]{1,0:T(8,128)}) %all-reduce.3.cloned.1.call-update) | async-done | bytes 131088 | tf_op jit(solution)/shard_map/psum | solution.py:69
  539.3 1.1 fusion.17
  540.4 0.7 fusion.14
  541.1 0.7 copy.11
  (7 shorter events, 0.0 us)
Async XLA Ops:
  7.2 12.8 %copy-start.2 = (f32[8,4096]{1,0:T(8,128)S(1)}, f32[8,4096]{1,0:T(8,128)}, u32[]{:S(2)}) copy-start(f32[8,4096]{1,0:T(8,128)} %param.10) | copy-start | bytes 393220
  7.2 12.8 %copy-start.3 = (s32[4096]{0:T(1024)S(1)}, s32[4096]{0:T(1024)}, u32[]{:S(2)}) copy-start(s32[4096]{0:T(1024)} %param.7) | copy-start | bytes 49156
  7.2 135.6 %copy-start.4 = (s32[8]{0:T(128)S(1)}, s32[8]{0:T(128)}, u32[]{:S(2)}) copy-start(s32[8]{0:T(128)} %param.8) | copy-start | bytes 100
  7.2 277.3 %all-to-all-start = ((f32[16,256,256]{2,1,0:T(8,128)}), f32[16,256,256]{2,1,0:T(8,128)}, u32[]{:S(2)}, u32[]{:S(2)}) async-start(f32[16,256,256]{2,1,0:T(8,128)} %bitcast.16), calls=%async_computation | async-start | bytes 8388608 | tf_op jit(solution)/shard_map/all_to_all | solution.py:47
  19.9 519.4 %all-reduce.3.cloned.1.call-start = ((), (), s32[]{:S(2)}) async-start(), calls=%async_computation.1 | async-start | bytes 262144 | tf_op jit(solution)/shard_map/psum | solution.py:69
  142.8 3.9 copy-start.1
  142.8 66.3 %copy-start.5 = (f32[8,256]{1,0:T(8,128)S(1)}, f32[8,256]{1,0:T(8,128)}, u32[]{:S(2)}) copy-start(f32[8,256]{1,0:T(8,128)} %param.11) | copy-start | bytes 24580
  142.8 141.6 %copy-start.6 = (s32[8]{0:T(128)S(1)}, s32[8]{0:T(128)}, u32[]{:S(2)}) copy-start(s32[8]{0:T(128)} %param.9) | copy-start | bytes 100
  289.9 4.2 copy-start
Sparse Core Ops, SparseCore 0:
  299.9 239.3 all-reduce.2
where the time goes:
time: 549 us
  blocking collectives  361 us (66%)
  waiting for transfers between devices  132 us (24%)
  matrix products  19.4 us (4%)
  between operations  14.2 us (3%)
  starting transfers between devices  12.8 us (2%)
  local copies, waits for them, and re-layouts  6.05 us (1%)
    psum x1, waiting for transfers between devices, local(): time_grad = lax.psum(weigh_rows(shortfall, relaid), ('unit', 'day'))  132 us
    psum x1, blocking collectives, local(): lax.psum((jnp.sum(raised, axis=1), jnp.sum(treated, axis=1), jnp.sum(cont...  123 us
    psum x1, blocking collectives, local(): unit_total = lax.psum(jnp.sum(updated, axis=1), ('unit', 'day'))  73 us
    psum x1, blocking collectives, local(): lax.psum((weigh_rows(weights, outcomes), weigh_rows(treated, outcomes)),...  60.7 us
    all_gather x1, blocking collectives, local(): lax.all_gather(time_logit, 'day', axis=1, tiled=True)  49.2 us
    all_gather x1, blocking collectives, local(): unit_weights = lax.all_gather(row_share, 'day', axis=1, tiled=True)  30 us
    all_gather x1, blocking collectives, local(): lax.all_gather(residual, 'day', axis=1, tiled=True)  25.8 us
    all_to_all x1, starting transfers between devices, local(): lax.all_to_all(outcomes, 'day', split_axis=0, concat_axis=1, tiled=True)  12.7 us
  transfers between devices with their start and end apart: 2, of which 1 were waited for; matrix products, arithmetic and copies ran while one was open for 2% of the time, Pallas kernels for 0%

commit v1 on v0

v1 whole, which is shorter than its diff:
```python
import functools

import jax
import jax.numpy as jnp
from jax import lax
from jax.experimental import pallas as pl
from jax.experimental.pallas import tpu as pltpu
from jax.sharding import PartitionSpec as P

MESH = pl.DeviceIdType.MESH
step_rate = 16.0
CHUNK = 256
LANES = 128
UNIT_SPLIT = (4, 4)
DAY_SPLIT = (4, 2, 2)
f32, bf16 = jnp.float32, jnp.bfloat16


def dot_nn(a, b):
    return jnp.dot(a, b, preferred_element_type=f32)


def dot_nt(a, b):
    return lax.dot_general(a, b, (((1,), (1,)), ((), ())), preferred_element_type=f32)


def halves(v):
    high = v.astype(bf16).astype(f32)
    return high, v - high


def to_row(col):
    groups = col.shape[0]
    row_id = lax.broadcasted_iota(jnp.int32, (groups, LANES), 0)
    lane_id = lax.broadcasted_iota(jnp.int32, (groups, LANES), 1)
    return jnp.sum(jnp.where(row_id == lane_id, col, 0.0), axis=0, keepdims=True)


def to_col(row, groups):
    row_id = lax.broadcasted_iota(jnp.int32, (groups, LANES), 0)
    lane_id = lax.broadcasted_iota(jnp.int32, (groups, LANES), 1)
    return jnp.sum(jnp.where(row_id == lane_id, row, 0.0), axis=1, keepdims=True)


def column(ref, groups):
    row_id = lax.broadcasted_iota(jnp.int32, (groups, 1), 0)
    out = jnp.zeros((groups, 1), jnp.int32)
    for g in range(groups):
        out = jnp.where(row_id == g, ref[g], out)
    return out


class Exchange:
    def __init__(self, buf, send_sem, recv_sem, rank, size, place):
        self.buf, self.send_sem, self.recv_sem = buf, send_sem, recv_sem
        self.rank, self.size, self.place = rank, size, place
        self.sent = []

    def copy(self, k, src, dst, peer):
        return pltpu.make_async_remote_copy(
            src_ref=src, dst_ref=dst, send_sem=self.send_sem.at[k - 1], recv_sem=self.recv_sem.at[k - 1],
            device_id=self.place(peer), device_id_type=MESH,
        )

    def start(self, source=None):
        own = self.buf.at[self.rank]
        for k in range(1, self.size):
            peer = lax.rem(self.rank + k, self.size)
            copy = self.copy(k, own if source is None else source.at[peer], own, peer)
            copy.start()
            self.sent.append(copy)

    def wait(self):
        for k in range(1, self.size):
            peer = lax.rem(self.rank + self.size - k, self.size)
            slot = self.buf.at[peer]
            self.copy(k, slot, slot, peer).wait_recv()

    def drain(self):
        for copy in self.sent:
            copy.wait_send()

    def total(self):
        out = self.buf[0]
        for i in range(1, self.size):
            out = out + self.buf[i]
        return out


def kernel(
    unit_split, day_split,
    pre_ref, post_ref, x_hbm, cohort_ref, unit_logit_ref, time_logit_ref,
    unit_out, time_out,
    x_buf, high_buf, low_buf, left_buf, raised_buf, control_buf,
    ux_buf, uz_buf, gx_buf, gz_buf,
    upart, urs, uzh, uag, tpart, tpost, trs, tzh, tag, lam_buf, utot, ttot,
    x_sem, ux_s, ux_r, uz_s, uz_r, gx_s, gx_r, gz_s, gz_r,
    urs_s, urs_r, uzh_s, uzh_r, uag_s, uag_r, trs_s, trs_r, tzh_s, tzh_r, tag_s, tag_r,
    lam_s, lam_r, utot_s, utot_r, ttot_s, ttot_r,
):
    nx, nz = unit_split
    ny, nh, nc = day_split
    unit_n, day_n, shards = nx * nz, ny * nh * nc, ny * nc
    units, days = x_buf.shape
    groups = unit_logit_ref.shape[0]
    chunks = units // CHUNK
    shard = units // shards
    all_count = day_n * days

    u, d = lax.axis_index("unit"), lax.axis_index("day")
    ux, uz = lax.div(u, nz), lax.rem(u, nz)
    dy, dh, dc = lax.div(d, nh * nc), lax.rem(lax.div(d, nc), nh), lax.rem(d, nc)
    j = dy * nc + dc

    loads = []
    for k in range(chunks):
        rows = pl.ds(k * CHUNK, CHUNK)
        load = pltpu.make_async_copy(x_hbm.at[rows], x_buf.at[rows], x_sem.at[k])
        load.start()
        loads.append(load)

    barrier = pltpu.get_barrier_semaphore()
    for k in range(1, unit_n):
        pl.semaphore_signal(barrier, inc=1, device_id={"unit": lax.rem(u + k, unit_n)}, device_id_type=MESH)
    for k in range(1, day_n):
        pl.semaphore_signal(barrier, inc=1, device_id={"day": lax.rem(d + k, day_n)}, device_id_type=MESH)

    def in_shards(rank):
        return {"day": lax.div(rank, nc) * (nh * nc) + dh * nc + lax.rem(rank, nc)}

    def in_high(rank):
        return {"day": dy * (nh * nc) + rank * nc + dc}

    on_x = lambda rank: {"unit": rank * nz + uz}
    on_z = lambda rank: {"unit": ux * nz + rank}
    on_unit = lambda rank: {"unit": rank}
    on_day = lambda rank: {"day": rank}

    sum_x = Exchange(ux_buf, ux_s, ux_r, ux, nx, on_x)
    sum_z = Exchange(uz_buf, uz_s, uz_r, uz, nz, on_z)
    grad_x = Exchange(gx_buf, gx_s, gx_r, ux, nx, on_x)
    grad_z = Exchange(gz_buf, gz_s, gz_r, uz, nz, on_z)
    unit_rs = Exchange(urs, urs_s, urs_r, j, shards, in_shards)
    unit_zh = Exchange(uzh, uzh_s, uzh_r, dh, nh, in_high)
    unit_ag = Exchange(uag, uag_s, uag_r, j, shards, in_shards)
    time_rs = Exchange(trs, trs_s, trs_r, j, shards, in_shards)
    time_zh = Exchange(tzh, tzh_s, tzh_r, dh, nh, in_high)
    time_ag = Exchange(tag, tag_s, tag_r, j, shards, in_shards)
    lam_tot = Exchange(lam_buf, lam_s, lam_r, d, day_n, on_day)
    unit_tot = Exchange(utot, utot_s, utot_r, u, unit_n, on_unit)
    time_tot = Exchange(ttot, ttot_s, ttot_r, d, day_n, on_day)

    pre_end, post_start = column(pre_ref, groups), column(post_ref, groups)
    before_len = pre_end.astype(f32)
    after_len = (all_count - post_start).astype(f32)
    labels = lax.broadcasted_iota(jnp.int32, (groups, units), 0)
    cohort = jnp.broadcast_to(cohort_ref[...], (groups, units))
    treated = jnp.where(cohort == labels, 1.0, 0.0)
    control = jnp.where(cohort > labels, 1.0, 0.0)
    raised = jnp.exp(unit_logit_ref[...]) * control
    for i in range(shards):
        raised_buf[i] = raised[:, i * shard:(i + 1) * shard]
        control_buf[i] = control[:, i * shard:(i + 1) * shard]
    raised_high, raised_low = halves(raised)
    left_buf[...] = jnp.concatenate(
        [raised_high, raised_low, treated, jnp.zeros_like(treated)], axis=0
    ).astype(bf16)
    norm_part = jnp.sum(raised, axis=1, keepdims=True)
    treat_part = jnp.sum(treated, axis=1, keepdims=True)
    ctrl_part = jnp.sum(control, axis=1, keepdims=True)
    lane = lax.broadcasted_iota(jnp.int32, (groups, LANES), 1)
    stats = jnp.where(lane == 0, norm_part, jnp.where(lane == 1, treat_part, jnp.where(lane == 2, ctrl_part, 0.0)))

    day_index = d * days + lax.broadcasted_iota(jnp.int32, (groups, days), 1)
    before = jnp.where(day_index < pre_end, 1.0, 0.0)
    after = jnp.where(day_index >= post_start, 1.0, 0.0)
    time_raised = jnp.exp(time_logit_ref[...]) * before
    lam_buf[d] = to_row(jnp.sum(time_raised, axis=1, keepdims=True))
    time_high, time_low = halves(time_raised)
    time_left = jnp.concatenate([time_high, time_low, after, jnp.zeros_like(after)], axis=0).astype(bf16)

    acc = jnp.zeros((4 * groups, days), f32)
    for k in range(chunks):
        rows = pl.ds(k * CHUNK, CHUNK)
        loads[k].wait()
        part = x_buf[rows, :]
        high = part.astype(bf16)
        low = (part - high.astype(f32)).astype(bf16)
        high_buf[rows, :] = high
        low_buf[rows, :] = low
        left = left_buf[:, k * CHUNK:(k + 1) * CHUNK]
        acc = acc + dot_nn(left, high) + dot_nn(left, low)
    own = ux_buf.at[ux]
    own[:, 0:days] = acc[0:groups] + acc[groups:2 * groups]
    own[:, days:2 * days] = acc[2 * groups:3 * groups]
    own[:, 2 * days:] = stats

    pl.semaphore_wait(barrier, unit_n + day_n - 2)
    sum_x.start()
    lam_tot.start()

    for k in range(chunks):
        rows = pl.ds(k * CHUNK, CHUNK)
        out = dot_nt(time_left, high_buf[rows, :]) + dot_nt(time_left, low_buf[rows, :])
        i, at = (k * CHUNK) // shard, (k * CHUNK) % shard
        tpart[i, :, at:at + CHUNK] = out[0:groups] + out[groups:2 * groups]
        tpost[i, :, at:at + CHUNK] = out[2 * groups:3 * groups]

    sum_x.wait()
    uz_buf[uz] = sum_x.total()
    sum_z.start()

    lam_tot.wait()
    lam_sum = to_col(lam_tot.total(), groups)
    tpart[...] = tpart[...] / lam_sum[None] - tpost[...] / after_len[None]
    trs[j] = tpart[j]
    time_rs.start(tpart)

    sum_z.wait()
    sums = sum_z.total()
    unit_norm = sums[:, 2 * days:2 * days + 1]
    treat_count = jnp.maximum(sums[:, 2 * days + 1:2 * days + 2], 1.0)
    ctrl_count = sums[:, 2 * days + 2:2 * days + 3]
    residual = (sums[:, 0:days] / unit_norm - sums[:, days:2 * days] / treat_count) * before
    res_left = jnp.concatenate(halves(residual), axis=0).astype(bf16)
    for k in range(chunks):
        rows = pl.ds(k * CHUNK, CHUNK)
        out = dot_nt(res_left, high_buf[rows, :]) + dot_nt(res_left, low_buf[rows, :])
        i, at = (k * CHUNK) // shard, (k * CHUNK) % shard
        upart[i, :, at:at + CHUNK] = out[0:groups] + out[groups:2 * groups]
    urs[j] = upart[j]
    unit_rs.start(upart)

    time_rs.wait()
    tzh[dh] = time_rs.total()
    time_zh.start()
    unit_rs.wait()
    uzh[dh] = unit_rs.total()
    unit_zh.start()

    time_zh.wait()
    tag[j] = time_zh.total() * control_buf[j]
    time_ag.start()
    unit_zh.wait()
    uag[j] = raised_buf[j] / unit_norm * jnp.exp(-step_rate * unit_zh.total() / jnp.sqrt(before_len))
    unit_ag.start()

    time_ag.wait()
    acc = jnp.zeros((2 * groups, days), f32)
    for k in range(chunks):
        rows = pl.ds(k * CHUNK, CHUNK)
        i, at = (k * CHUNK) // shard, (k * CHUNK) % shard
        left = jnp.concatenate(halves(tag[i, :, at:at + CHUNK]), axis=0).astype(bf16)
        acc = acc + dot_nn(left, high_buf[rows, :]) + dot_nn(left, low_buf[rows, :])
    gx_buf[ux] = acc[0:groups] + acc[groups:2 * groups]
    grad_x.start()

    unit_ag.wait()
    folded = unit_ag.total()
    utot[u] = to_row(jnp.sum(folded, axis=1, keepdims=True))
    unit_tot.start()

    grad_x.wait()
    gz_buf[uz] = grad_x.total()
    grad_z.start()

    unit_tot.wait()
    unit_total = to_col(unit_tot.total(), groups)
    for i in range(shards):
        unit_out[:, i * shard:(i + 1) * shard] = uag[i] / unit_total * ctrl_count

    grad_z.wait()
    ctrl_root = jnp.sqrt(jnp.maximum(ctrl_count, 1.0))
    moved = time_raised / lam_sum * jnp.exp(-step_rate * grad_z.total() / ctrl_root)
    ttot[d] = to_row(jnp.sum(moved, axis=1, keepdims=True))
    time_tot.start()
    time_tot.wait()
    time_out[...] = moved / to_col(time_tot.total(), groups) * before_len

    for group in (
        sum_x, lam_tot, sum_z, time_rs, unit_rs, time_zh, unit_zh, time_ag, unit_ag, grad_x, unit_tot, grad_z, time_tot
    ):
        group.drain()


def local(unit_split, day_split, outcomes, cohort, pre_end, post_start, unit_logit, time_logit):
    groups = pre_end.shape[0]
    units, days = outcomes.shape
    nx, nz = unit_split
    ny, nh, nc = day_split
    shards = ny * nc
    shard = units // shards
    wide = 2 * days + LANES
    vmem = pl.BlockSpec(memory_space=pltpu.VMEM)
    smem = pl.BlockSpec(memory_space=pltpu.SMEM)
    dma = lambda n: pltpu.SemaphoreType.DMA((n,))
    pairs = lambda *sizes: [dma(n - 1) for n in sizes for _ in range(2)]
    slots = lambda n: pltpu.VMEM((n, groups, shard), f32)
    return pl.pallas_call(
        functools.partial(kernel, unit_split, day_split),
        out_shape=(
            jax.ShapeDtypeStruct((groups, units), f32),
            jax.ShapeDtypeStruct((groups, days), f32),
        ),
        in_specs=[smem, smem, pl.BlockSpec(memory_space=pl.ANY), vmem, vmem, vmem],
        out_specs=(vmem, vmem),
        scratch_shapes=[
            pltpu.VMEM((units, days), f32),
            pltpu.VMEM((units, days), bf16),
            pltpu.VMEM((units, days), bf16),
            pltpu.VMEM((4 * groups, units), bf16),
            slots(shards), slots(shards),
            pltpu.VMEM((nx, groups, wide), f32),
            pltpu.VMEM((nz, groups, wide), f32),
            pltpu.VMEM((nx, groups, days), f32),
            pltpu.VMEM((nz, groups, days), f32),
            slots(shards), slots(shards), slots(nh), slots(shards),
            slots(shards), slots(shards), slots(shards), slots(nh), slots(shards),
            pltpu.VMEM((ny * nh * nc, 1, LANES), f32),
            pltpu.VMEM((nx * nz, 1, LANES), f32),
            pltpu.VMEM((ny * nh * nc, 1, LANES), f32),
            dma(units // CHUNK),
            *pairs(nx, nz, nx, nz),
            *pairs(shards, nh, shards, shards, nh, shards),
            *pairs(ny * nh * nc, nx * nz, ny * nh * nc),
        ],
        compiler_params=pltpu.CompilerParams(collective_id=0, has_side_effects=True),
    )(pre_end, post_start, outcomes, cohort.reshape(1, units), unit_logit, time_logit)


def solution(mesh):
    return jax.shard_map(
        functools.partial(local, UNIT_SPLIT, DAY_SPLIT),
        mesh=mesh,
        in_specs=(P("unit", "day"), P("unit"), P(), P(), P(None, "unit"), P(None, "day")),
        out_specs=(P(None, "unit"), P(None, "day")),
        check_vma=False,
    )
```

time: 549 us -> 50.9 us (0.09)
  blocking collectives: 361 us -> 0 us
  waiting for transfers between devices: 132 us -> 0 us
  Pallas kernels: 0 us -> 47.2 us
  matrix products: 19.4 us -> 0 us
  between operations: 14.2 us -> 0.64 us
  starting transfers between devices: 12.8 us -> 0 us
    psum x3 -> x0, blocking collectives: 256 us -> none  [the longest x1 123 us: local(): lax.psum((jnp.sum(raised, axis=1), jnp.sum(treated, axis=1), jnp.sum(cont...]
    psum x1 -> x0, waiting for transfers between devices: 132 us -> none  [local(): time_grad = lax.psum(weigh_rows(shortfall, relaid), ('unit', 'day'))]
    all_gather x3 -> x0, blocking collectives: 105 us -> none  [the longest x1 49.2 us: local(): lax.all_gather(time_logit, 'day', axis=1, tiled=True)]
    pallas_call x0 -> x1, Pallas kernels: none -> 47.2 us  [local(): pl.pallas_call(functools.partial(kernel, unit_split, day_split), out_shap...]
    dot_general x6 -> x0, matrix products: 19.4 us -> none  [the longest x3 9.75 us: weigh_rows(): jnp.dot(left, outcomes, precision=highest, preferred_element_type=jnp.flo...]
    all_to_all x1 -> x0, starting transfers between devices: 12.7 us -> none  [local(): lax.all_to_all(outcomes, 'day', split_axis=0, concat_axis=1, tiled=True)]
  transfers between devices with their start and end apart: 2 -> 0, of which waited for: 1 -> 0; matrix products, arithmetic and copies ran while one was open for 2% -> 0% of each run, Pallas kernels for 0% -> 0%
where the time goes in v1:
time: 50.9 us; the launch traced here: 50.7 us
  Pallas kernels  47.2 us (93%)
  local copies, waits for them, and re-layouts  2.86 us (6%)
  between operations  0.64 us (1%)
    pallas_call x1, Pallas kernels, local(): pl.pallas_call(functools.partial(kernel, unit_split, day_split), out_shap...  47.2 us
    unnamed x2, local copies, waits for them, and re-layouts  2.86 us

profile of v1, /device:TPU:1, one launch (start us, length us, event | category | flops | bytes accessed | tf_op | source)
XLA Modules:
  0.0 50.7 jit_solution(752413363710016458)
XLA Ops:
  0.6 47.2 %shard_map.77 = (f32[8,4096]{1,0:T(8,128)}, f32[8,256]{1,0:T(8,128)}) custom-call(s32[8]{0:T(128)} %pre_ref.1, s32[8]{0:T(128)} %post_ref.1, f32[4096,256]{1,0:T(8,128)} %x_hbm.1, s32[1,4096]{1,0:T(1,128)} %bitcast.1, f32[8,4096]{1,0:T(8,128)} %unit_logit_ref.1, f32[8,256]{1,0:T(8,128)} %time_logit_ref.1), custom_call_target="tpu_custom_call" | custom-call | tf_op jit(solution)/shard_map/pallas_call | solution.py:299
  47.8 1.6 %copy.10 = f32[8,4096]{1,0:T(8,128)} copy(f32[8,4096]{1,0:T(8,128)} %get-tuple-element.4) | data formatting | bytes 262144
  49.4 1.3 %copy.11 = f32[8,256]{1,0:T(8,128)} copy(f32[8,256]{1,0:T(8,128)} %get-tuple-element.5) | data formatting | bytes 16384

commit v2 on v1

v2 whole, which is shorter than its diff:
```python
import functools

import jax
import jax.numpy as jnp
from jax import lax
from jax.experimental import pallas as pl
from jax.experimental.pallas import tpu as pltpu
from jax.sharding import PartitionSpec as P

MESH = pl.DeviceIdType.MESH
step_rate = 16.0
CHUNK = 256
LANES = 128
UNIT_SPLIT = (4, 4)
DAY_SPLIT = (4, 2, 2)
f32, bf16 = jnp.float32, jnp.bfloat16


def dot_nn(a, b):
    return jnp.dot(a, b, preferred_element_type=f32)


def dot_nt(a, b):
    return lax.dot_general(a, b, (((1,), (1,)), ((), ())), preferred_element_type=f32)


def halves(v):
    high = v.astype(bf16).astype(f32)
    return high, v - high


def to_row(col):
    groups = col.shape[0]
    row_id = lax.broadcasted_iota(jnp.int32, (groups, LANES), 0)
    lane_id = lax.broadcasted_iota(jnp.int32, (groups, LANES), 1)
    return jnp.sum(jnp.where(row_id == lane_id, col, 0.0), axis=0, keepdims=True)


def to_col(row, groups):
    row_id = lax.broadcasted_iota(jnp.int32, (groups, LANES), 0)
    lane_id = lax.broadcasted_iota(jnp.int32, (groups, LANES), 1)
    return jnp.sum(jnp.where(row_id == lane_id, row, 0.0), axis=1, keepdims=True)


def column(ref, groups):
    row_id = lax.broadcasted_iota(jnp.int32, (groups, 1), 0)
    out = jnp.zeros((groups, 1), jnp.int32)
    for g in range(groups):
        out = jnp.where(row_id == g, ref[g], out)
    return out


class Exchange:
    def __init__(self, buf, send_sem, recv_sem, rank, size, place, sends=None, takes=None):
        self.buf, self.send_sem, self.recv_sem = buf, send_sem, recv_sem
        self.rank, self.size, self.place = rank, size, place
        self.sends, self.takes = sends, takes

    def copy(self, k, src, dst, peer):
        return pltpu.make_async_remote_copy(
            src_ref=src, dst_ref=dst, send_sem=self.send_sem.at[k - 1], recv_sem=self.recv_sem.at[k - 1],
            device_id=self.place(peer), device_id_type=MESH,
        )

    def over_sends(self, act):
        for k in range(1, self.size):
            peer = lax.rem(self.rank + k, self.size)
            if self.takes is None:
                act(k, peer)
            else:
                pl.when(self.takes(peer))(functools.partial(act, k, peer))

    def start(self, source=None):
        own = self.buf.at[self.rank]

        def act(k, peer):
            self.copy(k, own if source is None else source.at[peer], own, peer).start()

        self.over_sends(act)

    def drain(self):
        own = self.buf.at[self.rank]
        self.over_sends(lambda k, peer: self.copy(k, own, own, peer).wait_send())

    def wait(self):
        for k in range(1, self.size):
            peer = lax.rem(self.rank + self.size - k, self.size)

            def act(k=k, peer=peer):
                slot = self.buf.at[peer]
                self.copy(k, slot, slot, peer).wait_recv()

            if self.sends is None:
                act()
            else:
                pl.when(self.sends(peer))(act)

    def total(self, low=0, high=None):
        out = self.buf[low]
        for i in range(low + 1, self.size if high is None else high):
            out = out + self.buf[i]
        return out


def kernel(
    unit_split, day_split,
    pre_hbm, post_hbm, x_hbm, cohort_hbm, unit_logit_hbm, time_logit_hbm,
    unit_out, time_out,
    pre_ref, post_ref, cohort_ref, unit_logit_ref, time_logit_ref,
    x_buf, high_buf, low_buf, left_buf, raised_buf, control_buf, moved_buf, stat_buf,
    ux_buf, uz_buf, gx_buf, gz_buf,
    upart, urs, uzh, uag, tpart, trs, tzh, tag, utot, ttot,
    in_sem, x_sem, ux_s, ux_r, uz_s, uz_r, gx_s, gx_r, gz_s, gz_r,
    urs_s, urs_r, uzh_s, uzh_r, uag_s, uag_r, trs_s, trs_r, tzh_s, tzh_r, tag_s, tag_r,
    utot_s, utot_r, ttot_s, ttot_r,
):
    nx, nz = unit_split
    ny, nh, nc = day_split
    unit_n, day_n, shards = nx * nz, ny * nh * nc, ny * nc
    units, days = x_buf.shape
    groups = unit_logit_ref.shape[0]
    chunks = units // CHUNK
    shard = units // shards
    all_count = day_n * days
    early_ranks, early_days = shards // 2, day_n // 2

    u, d = lax.axis_index("unit"), lax.axis_index("day")
    ux, uz = lax.div(u, nz), lax.rem(u, nz)
    dy, dh, dc = lax.div(d, nh * nc), lax.rem(lax.div(d, nc), nh), lax.rem(d, nc)
    j = dy * nc + dc
    early = j < early_ranks

    barrier = pltpu.get_barrier_semaphore()
    for k in range(1, unit_n):
        pl.semaphore_signal(barrier, inc=1, device_id={"unit": lax.rem(u + k, unit_n)}, device_id_type=MESH)
    for k in range(1, day_n):
        pl.semaphore_signal(barrier, inc=1, device_id={"day": lax.rem(d + k, day_n)}, device_id_type=MESH)

    inputs = []
    for k, (src, dst) in enumerate((
        (time_logit_hbm, time_logit_ref), (pre_hbm, pre_ref), (post_hbm, post_ref),
        (unit_logit_hbm, unit_logit_ref), (cohort_hbm, cohort_ref),
    )):
        inputs.append(pltpu.make_async_copy(src, dst, in_sem.at[k]))
    loads = []
    for k in range(chunks):
        rows = pl.ds(k * CHUNK, CHUNK)
        loads.append(pltpu.make_async_copy(x_hbm.at[rows], x_buf.at[rows], x_sem.at[k]))
    for copy in inputs[:3] + loads[:2] + inputs[3:] + loads[2:]:
        copy.start()

    def in_shards(rank):
        return {"day": lax.div(rank, nc) * (nh * nc) + dh * nc + lax.rem(rank, nc)}

    def in_high(rank):
        return {"day": dy * (nh * nc) + rank * nc + dc}

    on_x = lambda rank: {"unit": rank * nz + uz}
    on_z = lambda rank: {"unit": ux * nz + rank}
    on_unit = lambda rank: {"unit": rank}
    on_day = lambda rank: {"day": rank}
    is_early = lambda rank: rank < early_ranks

    sum_x = Exchange(ux_buf, ux_s, ux_r, ux, nx, on_x)
    sum_z = Exchange(uz_buf, uz_s, uz_r, uz, nz, on_z)
    grad_x = Exchange(gx_buf, gx_s, gx_r, ux, nx, on_x)
    grad_z = Exchange(gz_buf, gz_s, gz_r, uz, nz, on_z)
    unit_rs = Exchange(urs, urs_s, urs_r, j, shards, in_shards, sends=is_early)
    unit_zh = Exchange(uzh, uzh_s, uzh_r, dh, nh, in_high)
    unit_ag = Exchange(uag, uag_s, uag_r, j, shards, in_shards)
    time_rs = Exchange(trs, trs_s, trs_r, j, shards, in_shards)
    time_zh = Exchange(tzh, tzh_s, tzh_r, dh, nh, in_high)
    time_ag = Exchange(tag, tag_s, tag_r, j, shards, in_shards, takes=is_early)
    unit_tot = Exchange(utot, utot_s, utot_r, u, unit_n, on_unit)
    time_tot = Exchange(ttot, ttot_s, ttot_r, d, early_days, on_day)

    for copy in inputs[:3]:
        copy.wait()
    pre_end, post_start = column(pre_ref, groups), column(post_ref, groups)
    before_len = pre_end.astype(f32)
    after_len = (all_count - post_start).astype(f32)
    day_index = d * days + lax.broadcasted_iota(jnp.int32, (groups, days), 1)
    before = jnp.where(day_index < pre_end, 1.0, 0.0)
    after = jnp.where(day_index >= post_start, 1.0, 0.0)
    time_raised = jnp.exp(time_logit_ref[...]) * before
    moved_buf[...] = time_raised
    time_left = jnp.concatenate(halves(time_raised + after), axis=0).astype(bf16)
    scale = jnp.where(early, 1.0, 1.0 / after_len)
    lam_tile = jnp.broadcast_to(jnp.sum(time_raised, axis=1, keepdims=True), (groups, LANES))
    for i in range(shards):
        tpart[i, :, shard:] = lam_tile
    for k in range(chunks):
        rows = pl.ds(k * CHUNK, CHUNK)
        loads[k].wait()
        part = x_buf[rows, :]
        high = part.astype(bf16)
        low = (part - high.astype(f32)).astype(bf16)
        high_buf[rows, :] = high
        low_buf[rows, :] = low
        out = dot_nt(time_left, high) + dot_nt(time_left, low)
        i, at = (k * CHUNK) // shard, (k * CHUNK) % shard
        tpart[i, :, at:at + CHUNK] = (out[0:groups] + out[groups:]) * scale

    pl.semaphore_wait(barrier, unit_n + day_n - 2)
    trs[j] = tpart[j]
    time_rs.start(tpart)

    for copy in inputs[3:]:
        copy.wait()
    labels = lax.broadcasted_iota(jnp.int32, (groups, units), 0)
    cohort = jnp.broadcast_to(cohort_ref[...], (groups, units))
    treated = jnp.where(cohort == labels, 1.0, 0.0)
    control = jnp.where(cohort > labels, 1.0, 0.0)
    raised = jnp.exp(unit_logit_ref[...]) * control
    for i in range(shards):
        raised_buf[i] = raised[:, i * shard:(i + 1) * shard]
        control_buf[i] = control[:, i * shard:(i + 1) * shard]

    @pl.when(early)
    def _():
        raised_high, raised_low = halves(raised)
        left_buf[...] = jnp.concatenate(
            [raised_high, raised_low, treated, jnp.zeros_like(treated)], axis=0
        ).astype(bf16)
        norm_part = jnp.sum(raised, axis=1, keepdims=True)
        treat_part = jnp.sum(treated, axis=1, keepdims=True)
        ctrl_part = jnp.sum(control, axis=1, keepdims=True)
        lane = lax.broadcasted_iota(jnp.int32, (groups, LANES), 1)
        stats = jnp.where(
            lane == 0, norm_part, jnp.where(lane == 1, treat_part, jnp.where(lane == 2, ctrl_part, 0.0))
        )
        acc = dot_nn(left_buf[...], high_buf[...]) + dot_nn(left_buf[...], low_buf[...])
        own = ux_buf.at[ux]
        own[:, 0:days] = acc[0:groups] + acc[groups:2 * groups]
        own[:, days:2 * days] = acc[2 * groups:3 * groups]
        own[:, 2 * days:] = stats
        sum_x.start()

    time_rs.wait()
    own_zh = tzh.at[dh]
    own_zh[0] = time_rs.total(0, early_ranks)
    own_zh[1] = time_rs.total(early_ranks, shards)
    time_zh.start()

    @pl.when(early)
    def _():
        sum_x.wait()
        uz_buf[uz] = sum_x.total()
        sum_z.start()

    time_zh.wait()
    both = time_zh.total()
    lam_owner = both[0, :, shard:shard + 1]
    own_ag = tag.at[j]
    own_ag[:, 0:shard] = (both[0, :, 0:shard] / lam_owner - both[1, :, 0:shard]) * control_buf[j]
    own_ag[:, shard:] = both[0, :, shard:]
    time_ag.start()

    @pl.when(early)
    def _():
        sum_z.wait()
        sums = sum_z.total()
        unit_norm = sums[:, 2 * days:2 * days + 1]
        treat_count = jnp.maximum(sums[:, 2 * days + 1:2 * days + 2], 1.0)
        residual = (sums[:, 0:days] / unit_norm - sums[:, days:2 * days] / treat_count) * before
        res_left = jnp.concatenate(halves(residual), axis=0).astype(bf16)
        for i in range(shards):
            rows = pl.ds(i * shard, shard)
            out = dot_nt(res_left, high_buf[rows, :]) + dot_nt(res_left, low_buf[rows, :])
            upart[i, :, 0:shard] = out[0:groups] + out[groups:]
            upart[i, :, shard:] = sums[:, 2 * days:]
        urs[j] = upart[j]
        unit_rs.start(upart)

    @pl.when(early)
    def _():
        time_ag.wait()
        for i in range(shards):
            left_buf[0:2 * groups, i * shard:(i + 1) * shard] = jnp.concatenate(
                halves(tag[i, :, 0:shard]), axis=0
            ).astype(bf16)
        left = left_buf[0:2 * groups, :]
        acc = dot_nn(left, high_buf[...]) + dot_nn(left, low_buf[...])
        gx_buf[ux] = acc[0:groups] + acc[groups:]
        grad_x.start()

    unit_rs.wait()
    grads = unit_rs.total(0, early_ranks)
    uzh[dh] = grads[:, 0:shard]
    stat_buf[...] = urs[0, :, shard:]
    unit_zh.start()

    @pl.when(early)
    def _():
        grad_x.wait()
        gz_buf[uz] = grad_x.total()
        grad_z.start()

    unit_zh.wait()
    unit_norm = stat_buf[:, 0:1]
    ctrl_count = stat_buf[:, 2:3]
    uag[j] = raised_buf[j] / unit_norm * jnp.exp(-step_rate * unit_zh.total() / jnp.sqrt(before_len))
    unit_ag.start()

    @pl.when(early)
    def _():
        grad_z.wait()
        lam = moved_buf[...] / tag[0, :, shard:shard + 1]
        ctrl_root = jnp.sqrt(jnp.maximum(ctrl_count, 1.0))
        moved = lam * jnp.exp(-step_rate * grad_z.total() / ctrl_root)
        moved_buf[...] = moved
        ttot[d] = to_row(jnp.sum(moved, axis=1, keepdims=True))
        time_tot.start()

    unit_ag.wait()
    utot[u] = to_row(jnp.sum(unit_ag.total(), axis=1, keepdims=True))
    unit_tot.start()

    unit_tot.wait()
    unit_total = to_col(unit_tot.total(), groups)
    for i in range(shards):
        unit_out[:, i * shard:(i + 1) * shard] = uag[i] / unit_total * ctrl_count

    @pl.when(early)
    def _():
        time_tot.wait()
        time_out[...] = moved_buf[...] / to_col(time_tot.total(), groups) * before_len

    @pl.when(jnp.logical_not(early))
    def _():
        time_out[...] = jnp.zeros_like(time_out)

    for group in (time_rs, time_zh, time_ag, unit_zh, unit_ag, unit_tot):
        group.drain()

    @pl.when(early)
    def _():
        for group in (sum_x, sum_z, unit_rs, grad_x, grad_z, time_tot):
            group.drain()


def local(unit_split, day_split, outcomes, cohort, pre_end, post_start, unit_logit, time_logit):
    groups = pre_end.shape[0]
    units, days = outcomes.shape
    nx, nz = unit_split
    ny, nh, nc = day_split
    unit_n, day_n, shards = nx * nz, ny * nh * nc, ny * nc
    shard = units // shards
    wide = 2 * days + LANES
    vmem = pl.BlockSpec(memory_space=pltpu.VMEM)
    hbm = pl.BlockSpec(memory_space=pl.ANY)
    dma = lambda n: pltpu.SemaphoreType.DMA((n,))
    pairs = lambda *sizes: [dma(n - 1) for n in sizes for _ in range(2)]
    slots = lambda n, size: pltpu.VMEM((n, groups, size), f32)
    return pl.pallas_call(
        functools.partial(kernel, unit_split, day_split),
        out_shape=(
            jax.ShapeDtypeStruct((groups, units), f32),
            jax.ShapeDtypeStruct((groups, days), f32),
        ),
        in_specs=[hbm] * 6,
        out_specs=(vmem, vmem),
        scratch_shapes=[
            pltpu.SMEM((groups,), jnp.int32),
            pltpu.SMEM((groups,), jnp.int32),
            pltpu.VMEM((1, units), jnp.int32),
            pltpu.VMEM((groups, units), f32),
            pltpu.VMEM((groups, days), f32),
            pltpu.VMEM((units, days), f32),
            pltpu.VMEM((units, days), bf16),
            pltpu.VMEM((units, days), bf16),
            pltpu.VMEM((4 * groups, units), bf16),
            slots(shards, shard), slots(shards, shard),
            pltpu.VMEM((groups, days), f32),
            pltpu.VMEM((groups, LANES), f32),
            slots(nx, wide), slots(nz, wide), slots(nx, days), slots(nz, days),
            slots(shards, shard + LANES), slots(shards, shard + LANES), slots(nh, shard), slots(shards, shard),
            slots(shards, shard + LANES), slots(shards, shard + LANES),
            pltpu.VMEM((nh, 2, groups, shard + LANES), f32),
            slots(shards, shard + LANES),
            pltpu.VMEM((unit_n, 1, LANES), f32),
            pltpu.VMEM((day_n // 2, 1, LANES), f32),
            dma(5),
            dma(units // CHUNK),
            *pairs(nx, nz, nx, nz),
            *pairs(shards, nh, shards, shards, nh, shards),
            *pairs(unit_n, day_n // 2),
        ],
        compiler_params=pltpu.CompilerParams(collective_id=0, has_side_effects=True),
    )(pre_end, post_start, outcomes, cohort.reshape(1, units), unit_logit, time_logit)


def solution(mesh):
    return jax.shard_map(
        functools.partial(local, UNIT_SPLIT, DAY_SPLIT),
        mesh=mesh,
        in_specs=(P("unit", "day"), P("unit"), P(), P(), P(None, "unit"), P(None, "day")),
        out_specs=(P(None, "unit"), P(None, "day")),
        check_vma=False,
    )
```

time: 50.9 us -> 48.6 us (0.955)
  Pallas kernels: 47.2 us -> 44.9 us
    pallas_call x1, Pallas kernels: 47.2 us -> 44.9 us  [local(): pl.pallas_call(functools.partial(kernel, unit_split, day_split), out_shap...]
where the time goes in v2:
time: 48.6 us; the launch traced here: 48.4 us
  Pallas kernels  44.9 us (92%)
  local copies, waits for them, and re-layouts  2.86 us (6%)
  between operations  0.64 us (1%)
    pallas_call x1, Pallas kernels, local(): pl.pallas_call(functools.partial(kernel, unit_split, day_split), out_shap...  44.9 us
    unnamed x2, local copies, waits for them, and re-layouts  2.86 us

profile of v2, /device:TPU:1, one launch (start us, length us, event | category | flops | bytes accessed | tf_op | source)
XLA Modules:
  0.0 48.4 jit_solution(13504767469003200560)
XLA Ops:
  0.6 44.9 %shard_map.77 = (f32[8,4096]{1,0:T(8,128)}, f32[8,256]{1,0:T(8,128)}) custom-call(s32[8]{0:T(128)} %pre_hbm.1, s32[8]{0:T(128)} %post_hbm.1, f32[4096,256]{1,0:T(8,128)} %x_hbm.1, s32[1,4096]{1,0:T(1,128)} %bitcast.1, f32[8,4096]{1,0:T(8,128)} %unit_logit_hbm.1, f32[8,256]{1,0:T(8,128)} %time_logit_hbm.1), custom_call_target="tpu_custom_call" | custom-call | tf_op jit(solution)/shard_map/pallas_call | solution.py:355
  45.5 1.6 %copy.10 = f32[8,4096]{1,0:T(8,128)} copy(f32[8,4096]{1,0:T(8,128)} %get-tuple-element.4) | data formatting | bytes 262144
  47.1 1.3 %copy.11 = f32[8,256]{1,0:T(8,128)} copy(f32[8,256]{1,0:T(8,128)} %get-tuple-element.5) | data formatting | bytes 16384

commit v3 on v2

v3 whole, which is shorter than its diff:
```python
import functools

import jax
import jax.numpy as jnp
from jax import lax
from jax.experimental import pallas as pl
from jax.experimental.pallas import tpu as pltpu
from jax.sharding import PartitionSpec as P

MESH = pl.DeviceIdType.MESH
step_rate = 16.0
CHUNK = 256
LANES = 128
UNIT_SPLIT = (4, 4)
DAY_SPLIT = (4, 2, 2)
f32, bf16 = jnp.float32, jnp.bfloat16


def dot_nn(a, b):
    return jnp.dot(a, b, preferred_element_type=f32)


def dot_nt(a, b):
    return lax.dot_general(a, b, (((1,), (1,)), ((), ())), preferred_element_type=f32)


def halves(v):
    high = v.astype(bf16).astype(f32)
    return high, v - high


def to_row(col):
    groups = col.shape[0]
    row_id = lax.broadcasted_iota(jnp.int32, (groups, LANES), 0)
    lane_id = lax.broadcasted_iota(jnp.int32, (groups, LANES), 1)
    return jnp.sum(jnp.where(row_id == lane_id, col, 0.0), axis=0, keepdims=True)


def to_col(row, groups):
    row_id = lax.broadcasted_iota(jnp.int32, (groups, LANES), 0)
    lane_id = lax.broadcasted_iota(jnp.int32, (groups, LANES), 1)
    return jnp.sum(jnp.where(row_id == lane_id, row, 0.0), axis=1, keepdims=True)


def column(ref, groups):
    row_id = lax.broadcasted_iota(jnp.int32, (groups, 1), 0)
    out = jnp.zeros((groups, 1), jnp.int32)
    for g in range(groups):
        out = jnp.where(row_id == g, ref[g], out)
    return out


class Exchange:
    def __init__(self, buf, sems, rank, size, place, takes=None, flag=None, sent=None, taken=None):
        self.buf, self.sems = buf, sems
        self.rank, self.size, self.place = rank, size, place
        self.takes, self.flag = takes, flag
        self.sent = size - 1 if sent is None else sent
        self.taken = size - 1 if taken is None else taken

    def copy(self, src, dst, peer):
        return pltpu.make_async_remote_copy(
            src_ref=src, dst_ref=dst, send_sem=self.sems.at[0], recv_sem=self.sems.at[1],
            device_id=self.place(peer), device_id_type=MESH,
        )

    def start(self, source=None):
        own = self.buf.at[self.rank]
        for k in range(1, self.size):
            peer = lax.rem(self.rank + k, self.size)

            def act(peer=peer):
                self.copy(own if source is None else source.at[peer], own, peer).start()

            if self.takes is None:
                act()
            else:
                pl.when(self.takes(peer))(act)

    def all_of(self, count, act):
        def some(n):
            if n:
                slots = self.buf.at[pl.ds(0, n)]
                act(self.copy(slots, slots, lax.rem(self.rank + 1, self.size)))

        if isinstance(count, tuple):
            pl.when(self.flag)(lambda: some(count[0]))
            pl.when(jnp.logical_not(self.flag))(lambda: some(count[1]))
        else:
            some(count)

    def drain(self):
        self.all_of(self.sent, lambda copy: copy.wait_send())

    def wait(self):
        self.all_of(self.taken, lambda copy: copy.wait_recv())

    def total(self, low=0, high=None):
        out = self.buf[low]
        for i in range(low + 1, self.size if high is None else high):
            out = out + self.buf[i]
        return out


def kernel(
    unit_split, day_split,
    pre_hbm, post_hbm, x_hbm, cohort_hbm, unit_logit_hbm, time_logit_hbm,
    unit_out, time_out,
    pre_ref, post_ref, cohort_ref, unit_logit_ref, time_logit_ref,
    x_buf, high_buf, low_buf, high_turned, low_turned, left_buf, raised_buf, control_buf, moved_buf,
    stat_buf, ux_buf, uz_buf, grad,
    upart, urs, uzh, uag, tpart, trs, tzh, tag, lrs, lzh, utot, uall, ttot,
    in_sem, x_sem, stat_sem, ux_sem, uz_sem, grad_sem,
    urs_sem, uzh_sem, uag_sem, trs_sem, tzh_sem, tag_sem, lrs_sem, lzh_sem, utot_sem, uall_sem, ttot_sem,
):
    nx, nz = unit_split
    ny, nh, nc = day_split
    unit_n, day_n, shards = nx * nz, ny * nh * nc, ny * nc
    units, days = x_buf.shape
    groups = unit_logit_ref.shape[0]
    chunks = units // CHUNK
    shard = units // shards
    all_count = day_n * days
    early_ranks, early_days = shards // 2, day_n // 2

    u, d = lax.axis_index("unit"), lax.axis_index("day")
    ux, uz = lax.div(u, nz), lax.rem(u, nz)
    dy, dh, dc = lax.div(d, nh * nc), lax.rem(lax.div(d, nc), nh), lax.rem(d, nc)
    j = dy * nc + dc
    early = j < early_ranks

    def in_shards(rank):
        return {"day": lax.div(rank, nc) * (nh * nc) + dh * nc + lax.rem(rank, nc)}

    def in_high(rank):
        return {"day": dy * (nh * nc) + rank * nc + dc}

    on_unit = lambda rank: {"unit": rank}
    on_day = lambda rank: {"day": rank}
    on_x = lambda rank: {"unit": rank * nz + uz}
    on_z = lambda rank: {"unit": ux * nz + rank}

    barrier = pltpu.get_barrier_semaphore()
    for k in range(1, unit_n):
        pl.semaphore_signal(barrier, inc=1, device_id=on_unit(lax.rem(u + k, unit_n)), device_id_type=MESH)
    for k in range(1, shards):
        pl.semaphore_signal(barrier, inc=1, device_id=in_shards(lax.rem(j + k, shards)), device_id_type=MESH)
    for k in range(1, nh):
        for i in range(early_ranks):
            peer = lax.rem(dh + k, nh) * nc + i // nc * nh * nc + i % nc

            @pl.when(early)
            def _(peer=peer):
                pl.semaphore_signal(barrier, inc=1, device_id=on_day(peer), device_id_type=MESH)

        @pl.when(jnp.logical_not(early))
        def _(k=k):
            pl.semaphore_signal(barrier, inc=1, device_id=in_high(lax.rem(dh + k, nh)), device_id_type=MESH)

    inputs = []
    for k, (src, dst) in enumerate((
        (time_logit_hbm, time_logit_ref), (pre_hbm, pre_ref), (post_hbm, post_ref),
        (unit_logit_hbm, unit_logit_ref), (cohort_hbm, cohort_ref),
    )):
        inputs.append(pltpu.make_async_copy(src, dst, in_sem.at[k]))
    loads = []
    for k in range(chunks):
        rows = pl.ds(k * CHUNK, CHUNK)
        loads.append(pltpu.make_async_copy(x_hbm.at[rows], x_buf.at[rows], x_sem.at[k]))
    for copy in inputs[:3] + loads + inputs[3:]:
        copy.start()

    stats = Exchange(stat_buf, stat_sem, u, unit_n, on_unit)
    sum_x = Exchange(ux_buf, ux_sem, ux, nx, on_x)
    sum_z = Exchange(uz_buf, uz_sem, uz, nz, on_z)
    to_early = (early_ranks - 1, early_ranks)
    from_early = dict(flag=early, taken=to_early)
    unit_rs = Exchange(urs, urs_sem, j, shards, in_shards, **from_early)
    unit_zh = Exchange(uzh, uzh_sem, dh, nh, in_high)
    unit_ag = Exchange(uag, uag_sem, j, shards, in_shards)
    unit_tot = Exchange(utot, utot_sem, u, unit_n, on_unit)
    unit_all = Exchange(uall, uall_sem, j, shards, in_shards)
    time_rs = Exchange(trs, trs_sem, j, shards, in_shards)
    time_zh = Exchange(tzh, tzh_sem, dh, nh, in_high)
    time_ag = Exchange(
        tag, tag_sem, j, shards, in_shards, takes=lambda rank: rank < early_ranks, flag=early, sent=to_early
    )
    lam_rs = Exchange(lrs, lrs_sem, j, shards, in_shards, **from_early)
    lam_zh = Exchange(lzh, lzh_sem, dh, nh, in_high)
    time_grad = Exchange(grad, grad_sem, u, unit_n, on_unit)
    time_tot = Exchange(ttot, ttot_sem, d, early_days, on_day)

    def split(k):
        rows = pl.ds(k * CHUNK, CHUNK)
        part = x_buf[rows, :]
        high = part.astype(bf16)
        high_buf[rows, :] = high
        low_buf[rows, :] = (part - high.astype(f32)).astype(bf16)

    half = chunks // 2
    for k in range(half):
        loads[k].wait()
        split(k)
    for copy in inputs[:3]:
        copy.wait()
    pre_end, post_start = column(pre_ref, groups), column(post_ref, groups)
    before_len = pre_end.astype(f32)
    after_len = (all_count - post_start).astype(f32)
    day_index = d * days + lax.broadcasted_iota(jnp.int32, (groups, days), 1)
    before = jnp.where(day_index < pre_end, 1.0, 0.0)
    after = jnp.where(day_index >= post_start, 1.0, 0.0)
    time_raised = jnp.exp(time_logit_ref[...]) * before
    moved_buf[...] = time_raised
    time_left = jnp.concatenate(halves(time_raised + after), axis=0).astype(bf16)
    scale = jnp.broadcast_to(jnp.where(early, 1.0, 1.0 / after_len), (groups, CHUNK))
    lrs[j] = to_row(jnp.sum(time_raised, axis=1, keepdims=True))

    def weigh(k):
        rows = pl.ds(k * CHUNK, CHUNK)
        out = dot_nt(time_left, high_buf[rows, :]) + dot_nt(time_left, low_buf[rows, :])
        i, at = (k * CHUNK) // shard, (k * CHUNK) % shard
        tpart[i, :, at:at + CHUNK] = (out[0:groups] + out[groups:]) * scale

    for k in range(half, chunks):
        loads[k].wait()
    for k in range(half):
        weigh(k)
        split(half + k)
    for k in range(half, chunks):
        weigh(k)

    pl.semaphore_wait(
        barrier, unit_n - 1 + shards - 1 + jnp.where(early, (nh - 1) * early_ranks, nh - 1)
    )
    trs[j] = tpart[j]
    time_rs.start(tpart)

    @pl.when(early)
    def _():
        lam_rs.start()

    for copy in inputs[3:]:
        copy.wait()
    labels = lax.broadcasted_iota(jnp.int32, (groups, units), 0)
    cohort = jnp.broadcast_to(cohort_ref[...], (groups, units))
    treated = jnp.where(cohort == labels, 1.0, 0.0)
    control = jnp.where(cohort > labels, 1.0, 0.0)
    raised = jnp.exp(unit_logit_ref[...]) * control
    for i in range(shards):
        raised_buf[i] = raised[:, i * shard:(i + 1) * shard]
        control_buf[i] = control[:, i * shard:(i + 1) * shard]
    norm_part = jnp.sum(raised, axis=1, keepdims=True)
    treat_part = jnp.sum(treated, axis=1, keepdims=True)
    ctrl_part = jnp.sum(control, axis=1, keepdims=True)
    rows3 = [to_row(norm_part), to_row(treat_part), to_row(ctrl_part)]
    stat_buf[u] = jnp.concatenate(rows3 + [jnp.zeros((groups - 3, LANES), f32)], axis=0)
    stats.start()

    @pl.when(early)
    def _():
        raised_high, raised_low = halves(raised)
        left_buf[...] = jnp.concatenate(
            [raised_high, raised_low, treated, jnp.zeros_like(treated)], axis=0
        ).astype(bf16)
        acc = dot_nn(left_buf[...], high_buf[...]) + dot_nn(left_buf[...], low_buf[...])
        ux_buf[ux, :, 0:days] = acc[0:groups] + acc[groups:2 * groups]
        ux_buf[ux, :, days:] = acc[2 * groups:3 * groups]
        sum_x.start()
        for k in range(chunks):
            rows = pl.ds(k * CHUNK, CHUNK)
            high_turned[:, k * CHUNK:(k + 1) * CHUNK] = high_buf[rows, :].T
            low_turned[:, k * CHUNK:(k + 1) * CHUNK] = low_buf[rows, :].T

    time_rs.wait()
    tzh[dh, 0] = time_rs.total(0, early_ranks)
    tzh[dh, 1] = time_rs.total(early_ranks, shards)
    time_zh.start()
    lam_rs.wait()
    lzh[dh] = lam_rs.total(0, early_ranks)
    lam_zh.start()

    @pl.when(early)
    def _():
        sum_x.wait()
        uz_buf[uz] = sum_x.total()
        sum_z.start()

    stats.wait()
    all_stats = stats.total()
    unit_norm = to_col(all_stats[0:1], groups)
    treat_count = jnp.maximum(to_col(all_stats[1:2], groups), 1.0)
    ctrl_count = to_col(all_stats[2:3], groups)

    @pl.when(early)
    def _():
        sum_z.wait()
        sums = sum_z.total()
        residual = (sums[:, 0:days] / unit_norm - sums[:, days:] / treat_count) * before
        res_left = jnp.concatenate(halves(residual), axis=0).astype(bf16)
        for i in range(shards):
            cols = slice(i * shard, (i + 1) * shard)
            out = dot_nn(res_left, high_turned[:, cols]) + dot_nn(res_left, low_turned[:, cols])
            upart[i] = out[0:groups] + out[groups:]
        urs[j] = upart[j]
        unit_rs.start(upart)

    time_zh.wait()
    lam_zh.wait()
    lam_sum = to_col(lam_zh.total(), groups)
    both = time_zh.total()
    tag[j] = (both[0] / lam_sum - both[1]) * control_buf[j]
    time_ag.start()

    unit_rs.wait()
    uzh[dh] = unit_rs.total(0, early_ranks)
    unit_zh.start()

    @pl.when(early)
    def _():
        time_ag.wait()
        for i in range(shards):
            left_buf[0:2 * groups, i * shard:(i + 1) * shard] = jnp.concatenate(
                halves(tag[i]), axis=0
            ).astype(bf16)
        left = left_buf[0:2 * groups, :]
        acc = dot_nn(left, high_buf[...]) + dot_nn(left, low_buf[...])
        grad[u] = acc[0:groups] + acc[groups:]
        time_grad.start()

    unit_zh.wait()
    updated = raised_buf[j] / unit_norm * jnp.exp(-step_rate * unit_zh.total() / jnp.sqrt(before_len))
    uag[j] = updated
    utot[u] = to_row(jnp.sum(updated, axis=1, keepdims=True))
    unit_tot.start()
    unit_ag.start()

    @pl.when(early)
    def _():
        time_grad.wait()
        ctrl_root = jnp.sqrt(jnp.maximum(ctrl_count, 1.0))
        moved = moved_buf[...] / lam_sum * jnp.exp(-step_rate * time_grad.total() / ctrl_root)
        moved_buf[...] = moved
        ttot[d] = to_row(jnp.sum(moved, axis=1, keepdims=True))
        time_tot.start()

    unit_tot.wait()
    uall[j] = unit_tot.total()
    unit_all.start()

    unit_ag.wait()
    unit_all.wait()
    unit_total = jnp.broadcast_to(to_col(unit_all.total(), groups), (groups, shard))
    count = jnp.broadcast_to(ctrl_count, (groups, shard))
    for i in range(shards):
        unit_out[:, i * shard:(i + 1) * shard] = uag[i] / unit_total * count

    @pl.when(early)
    def _():
        time_tot.wait()
        time_out[...] = moved_buf[...] / to_col(time_tot.total(), groups) * before_len

    @pl.when(jnp.logical_not(early))
    def _():
        time_out[...] = jnp.zeros_like(time_out)

    for group in (time_rs, stats, time_zh, lam_zh, time_ag, unit_zh, unit_ag, unit_tot, unit_all):
        group.drain()

    @pl.when(early)
    def _():
        for group in (lam_rs, sum_x, sum_z, unit_rs, time_grad, time_tot):
            group.drain()


def local(unit_split, day_split, outcomes, cohort, pre_end, post_start, unit_logit, time_logit):
    groups = pre_end.shape[0]
    units, days = outcomes.shape
    nx, nz = unit_split
    ny, nh, nc = day_split
    unit_n, day_n, shards = nx * nz, ny * nh * nc, ny * nc
    shard = units // shards
    hbm = pl.BlockSpec(memory_space=pl.ANY)
    vmem = pl.BlockSpec(memory_space=pltpu.VMEM)
    dma = lambda n: pltpu.SemaphoreType.DMA((n,))
    slots = lambda n, size: pltpu.VMEM((n, groups, size), f32)
    rows = lambda n: pltpu.VMEM((n, 1, LANES), f32)
    return pl.pallas_call(
        functools.partial(kernel, unit_split, day_split),
        out_shape=(pltpu.VMEM((groups, units), f32), pltpu.VMEM((groups, days), f32)),
        in_specs=[hbm] * 6,
        out_specs=(vmem, vmem),
        scratch_shapes=[
            pltpu.SMEM((groups,), jnp.int32),
            pltpu.SMEM((groups,), jnp.int32),
            pltpu.VMEM((1, units), jnp.int32),
            pltpu.VMEM((groups, units), f32),
            pltpu.VMEM((groups, days), f32),
            pltpu.VMEM((units, days), f32),
            pltpu.VMEM((units, days), bf16),
            pltpu.VMEM((units, days), bf16),
            pltpu.VMEM((days, units), bf16),
            pltpu.VMEM((days, units), bf16),
            pltpu.VMEM((4 * groups, units), bf16),
            slots(shards, shard), slots(shards, shard),
            pltpu.VMEM((groups, days), f32),
            slots(unit_n, LANES), slots(nx, 2 * days), slots(nz, 2 * days), slots(unit_n, days),
            slots(shards, shard), slots(shards, shard), slots(nh, shard), slots(shards, shard),
            slots(shards, shard), slots(shards, shard),
            pltpu.VMEM((nh, 2, groups, shard), f32),
            slots(shards, shard),
            rows(shards), rows(nh), rows(unit_n), rows(shards), rows(day_n // 2),
            dma(5),
            dma(units // CHUNK),
            *[dma(2)] * 15,
        ],
        compiler_params=pltpu.CompilerParams(collective_id=0, has_side_effects=True),
    )(pre_end, post_start, outcomes, cohort.reshape(1, units), unit_logit, time_logit)


def solution(mesh):
    return jax.shard_map(
        functools.partial(local, UNIT_SPLIT, DAY_SPLIT),
        mesh=mesh,
        in_specs=(P("unit", "day"), P("unit"), P(), P(), P(None, "unit"), P(None, "day")),
        out_specs=(P(None, "unit"), P(None, "day")),
        check_vma=False,
    )
```

time: 48.6 us -> 40.8 us (0.84)
  Pallas kernels: 44.9 us -> 38.8 us
  local copies, waits for them, and re-layouts: 2.86 us -> 1.26 us
    pallas_call x1, Pallas kernels: 44.9 us -> 38.8 us  [local(): pl.pallas_call(functools.partial(kernel, unit_split, day_split), out_shap...]
    unnamed x2, local copies, waits for them, and re-layouts: 2.86 us -> 1.26 us
where the time goes in v3:
time: 40.8 us; the launch traced here: 40.7 us
  Pallas kernels  38.8 us (95%)
  local copies, waits for them, and re-layouts  1.26 us (3%)
  between operations  0.64 us (2%)
    pallas_call x1, Pallas kernels, local(): pl.pallas_call(functools.partial(kernel, unit_split, day_split), out_shap...  38.8 us
    unnamed x2, local copies, waits for them, and re-layouts  1.26 us

profile of v3, /device:TPU:1, one launch (start us, length us, event | category | flops | bytes accessed | tf_op | source)
XLA Modules:
  0.0 40.7 jit_solution(9639850309174036057)
XLA Ops:
  0.6 38.8 %shard_map.77 = (f32[8,4096]{1,0:T(8,128)S(1)}, f32[8,256]{1,0:T(8,128)S(1)}) custom-call(s32[8]{0:T(128)} %pre_hbm.1, s32[8]{0:T(128)} %post_hbm.1, f32[4096,256]{1,0:T(8,128)} %x_hbm.1, s32[1,4096]{1,0:T(1,128)} %bitcast.1, f32[8,4096]{1,0:T(8,128)} %unit_logit_hbm.1, f32[8,256]{1,0:T(8,128)} %time_logit_hbm.1), custom_call_target="tpu_custom_call" | custom-call | tf_op jit(solution)/shard_map/pallas_call | solution.py:387
  39.5 0.7 %copy.10 = f32[8,4096]{1,0:T(8,128)} copy(f32[8,4096]{1,0:T(8,128)S(1)} %get-tuple-element.2) | data formatting | bytes 262144
  40.1 0.6 %copy.11 = f32[8,256]{1,0:T(8,128)} copy(f32[8,256]{1,0:T(8,128)S(1)} %get-tuple-element.3) | data formatting | bytes 16384

commit v4 on v3

--- a/solution.py
+++ b/solution.py
@@ -10,6 +10,7 @@
 MESH = pl.DeviceIdType.MESH
 step_rate = 16.0
 CHUNK = 256
+PARTS = 4
 LANES = 128
 UNIT_SPLIT = (4, 4)
 DAY_SPLIT = (4, 2, 2)
@@ -107,7 +108,7 @@
     pre_hbm, post_hbm, x_hbm, cohort_hbm, unit_logit_hbm, time_logit_hbm,
     unit_out, time_out,
     pre_ref, post_ref, cohort_ref, unit_logit_ref, time_logit_ref,
-    x_buf, high_buf, low_buf, high_turned, low_turned, left_buf, raised_buf, control_buf, moved_buf,
+    x_buf, high_buf, low_buf, high_turned, low_turned, left_buf, acc_buf, raised_buf, control_buf, moved_buf,
     stat_buf, ux_buf, uz_buf, grad,
     upart, urs, uzh, uag, tpart, trs, tzh, tag, lrs, lzh, utot, uall, ttot,
     in_sem, x_sem, stat_sem, ux_sem, uz_sem, grad_sem,
@@ -118,8 +119,8 @@
     unit_n, day_n, shards = nx * nz, ny * nh * nc, ny * nc
     units, days = x_buf.shape
     groups = unit_logit_ref.shape[0]
-    chunks = units // CHUNK
     shard = units // shards
+    own_units = units // (shards // 2)
     all_count = day_n * days
     early_ranks, early_days = shards // 2, day_n // 2
 
@@ -157,17 +158,19 @@
         def _(k=k):
             pl.semaphore_signal(barrier, inc=1, device_id=in_high(lax.rem(dh + k, nh)), device_id_type=MESH)
 
-    inputs = []
-    for k, (src, dst) in enumerate((
-        (time_logit_hbm, time_logit_ref), (pre_hbm, pre_ref), (post_hbm, post_ref),
-        (unit_logit_hbm, unit_logit_ref), (cohort_hbm, cohort_ref),
-    )):
-        inputs.append(pltpu.make_async_copy(src, dst, in_sem.at[k]))
-    loads = []
-    for k in range(chunks):
-        rows = pl.ds(k * CHUNK, CHUNK)
-        loads.append(pltpu.make_async_copy(x_hbm.at[rows], x_buf.at[rows], x_sem.at[k]))
-    for copy in inputs[:3] + loads + inputs[3:]:
+    inputs = [
+        pltpu.make_async_copy(src, dst, in_sem.at[k])
+        for k, (src, dst) in enumerate((
+            (unit_logit_hbm, unit_logit_ref), (cohort_hbm, cohort_ref), (time_logit_hbm, time_logit_ref),
+            (pre_hbm, pre_ref), (post_hbm, post_ref),
+        ))
+    ]
+    part = units // PARTS
+    loads = [
+        pltpu.make_async_copy(x_hbm.at[pl.ds(k * part, part)], x_buf.at[pl.ds(k * part, part)], x_sem.at[k])
+        for k in range(PARTS)
+    ]
+    for copy in inputs + loads:
         copy.start()
 
     stats = Exchange(stat_buf, stat_sem, u, unit_n, on_unit)
@@ -175,11 +178,11 @@
     sum_z = Exchange(uz_buf, uz_sem, uz, nz, on_z)
     to_early = (early_ranks - 1, early_ranks)
     from_early = dict(flag=early, taken=to_early)
-    unit_rs = Exchange(urs, urs_sem, j, shards, in_shards, **from_early)
+    unit_rs = Exchange(urs, urs_sem, j, early_ranks, in_shards)
     unit_zh = Exchange(uzh, uzh_sem, dh, nh, in_high)
-    unit_ag = Exchange(uag, uag_sem, j, shards, in_shards)
+    unit_ag = Exchange(uag, uag_sem, j, shards, in_shards, **from_early)
     unit_tot = Exchange(utot, utot_sem, u, unit_n, on_unit)
-    unit_all = Exchange(uall, uall_sem, j, shards, in_shards)
+    unit_all = Exchange(uall, uall_sem, j, shards, in_shards, **from_early)
     time_rs = Exchange(trs, trs_sem, j, shards, in_shards)
     time_zh = Exchange(tzh, tzh_sem, dh, nh, in_high)
     time_ag = Exchange(
@@ -190,19 +193,28 @@
     time_grad = Exchange(grad, grad_sem, u, unit_n, on_unit)
     time_tot = Exchange(ttot, ttot_sem, d, early_days, on_day)
 
-    def split(k):
-        rows = pl.ds(k * CHUNK, CHUNK)
-        part = x_buf[rows, :]
-        high = part.astype(bf16)
-        high_buf[rows, :] = high
-        low_buf[rows, :] = (part - high.astype(f32)).astype(bf16)
-
-    half = chunks // 2
-    for k in range(half):
-        loads[k].wait()
-        split(k)
-    for copy in inputs[:3]:
+    for copy in inputs:
         copy.wait()
+
+    labels = lax.broadcasted_iota(jnp.int32, (groups, units), 0)
+    cohort = jnp.broadcast_to(cohort_ref[...], (groups, units))
+    treated = jnp.where(cohort == labels, 1.0, 0.0)
+    control = jnp.where(cohort > labels, 1.0, 0.0)
+    raised = jnp.exp(unit_logit_ref[...]) * control
+    for i in range(shards):
+        control_buf[i] = control[:, i * shard:(i + 1) * shard]
+    for i in range(early_ranks):
+        raised_buf[i] = raised[:, i * own_units:(i + 1) * own_units]
+    raised_high, raised_low = halves(raised)
+    left_buf[...] = jnp.concatenate(
+        [raised_high, raised_low, treated, jnp.zeros_like(treated)], axis=0
+    ).astype(bf16)
+    norm_part = jnp.sum(raised, axis=1, keepdims=True)
+    treat_part = jnp.sum(treated, axis=1, keepdims=True)
+    ctrl_part = jnp.sum(control, axis=1, keepdims=True)
+    rows3 = [to_row(norm_part), to_row(treat_part), to_row(ctrl_part)]
+    stat_buf[u] = jnp.concatenate(rows3 + [jnp.zeros((groups - 3, LANES), f32)], axis=0)
+
     pre_end, post_start = column(pre_ref, groups), column(post_ref, groups)
     before_len = pre_end.astype(f32)
     after_len = (all_count - post_start).astype(f32)
@@ -212,26 +224,56 @@
     time_raised = jnp.exp(time_logit_ref[...]) * before
     moved_buf[...] = time_raised
     time_left = jnp.concatenate(halves(time_raised + after), axis=0).astype(bf16)
-    scale = jnp.broadcast_to(jnp.where(early, 1.0, 1.0 / after_len), (groups, CHUNK))
+    scale = jnp.broadcast_to(jnp.where(early, 1.0, 1.0 / after_len), (groups, shard))
     lrs[j] = to_row(jnp.sum(time_raised, axis=1, keepdims=True))
 
-    def weigh(k):
-        rows = pl.ds(k * CHUNK, CHUNK)
-        out = dot_nt(time_left, high_buf[rows, :]) + dot_nt(time_left, low_buf[rows, :])
-        i, at = (k * CHUNK) // shard, (k * CHUNK) % shard
-        tpart[i, :, at:at + CHUNK] = (out[0:groups] + out[groups:]) * scale
-
-    for k in range(half, chunks):
+    def split(k):
+        rows = pl.ds(k * part, part)
+        whole = x_buf[rows, :]
+        high = whole.astype(bf16)
+        high_buf[rows, :] = high
+        low_buf[rows, :] = (whole - high.astype(f32)).astype(bf16)
+
+    def weigh_units(k):
+        for i in range(k * part // shard, (k + 1) * part // shard):
+            rows = pl.ds(i * shard, shard)
+            out = dot_nt(time_left, high_buf[rows, :]) + dot_nt(time_left, low_buf[rows, :])
+            tpart[i] = (out[0:groups] + out[groups:]) * scale
+
+    def weigh_rows(k):
+        rows = pl.ds(k * part, part)
+        left = left_buf[:, k * part:(k + 1) * part]
+        return dot_nn(left, high_buf[rows, :]) + dot_nn(left, low_buf[rows, :])
+
+    for k in range(PARTS):
         loads[k].wait()
-    for k in range(half):
-        weigh(k)
-        split(half + k)
-    for k in range(half, chunks):
-        weigh(k)
+        split(k)
+
+        @pl.when(early)
+        def _(k=k):
+            acc = weigh_rows(k)
+            if k:
+                acc_buf[...] += acc
+            else:
+                acc_buf[...] = acc
+
+    @pl.when(early)
+    def _():
+        ux_buf[ux, :, 0:days] = acc_buf[0:groups] + acc_buf[groups:2 * groups]
+        ux_buf[ux, :, days:] = acc_buf[2 * groups:3 * groups]
+
+    for k in range(PARTS // 2):
+        weigh_units(k)
 
     pl.semaphore_wait(
         barrier, unit_n - 1 + shards - 1 + jnp.where(early, (nh - 1) * early_ranks, nh - 1)
     )
+    @pl.when(early)
+    def _():
+        sum_x.start()
+
+    for k in range(PARTS // 2, PARTS):
+        weigh_units(k)
     trs[j] = tpart[j]
     time_rs.start(tpart)
 
@@ -239,37 +281,17 @@
     def _():
         lam_rs.start()
 
-    for copy in inputs[3:]:
-        copy.wait()
-    labels = lax.broadcasted_iota(jnp.int32, (groups, units), 0)
-    cohort = jnp.broadcast_to(cohort_ref[...], (groups, units))
-    treated = jnp.where(cohort == labels, 1.0, 0.0)
-    control = jnp.where(cohort > labels, 1.0, 0.0)
-    raised = jnp.exp(unit_logit_ref[...]) * control
-    for i in range(shards):
-        raised_buf[i] = raised[:, i * shard:(i + 1) * shard]
-        control_buf[i] = control[:, i * shard:(i + 1) * shard]
-    norm_part = jnp.sum(raised, axis=1, keepdims=True)
-    treat_part = jnp.sum(treated, axis=1, keepdims=True)
-    ctrl_part = jnp.sum(control, axis=1, keepdims=True)
-    rows3 = [to_row(norm_part), to_row(treat_part), to_row(ctrl_part)]
-    stat_buf[u] = jnp.concatenate(rows3 + [jnp.zeros((groups - 3, LANES), f32)], axis=0)
     stats.start()
 
     @pl.when(early)
     def _():
-        raised_high, raised_low = halves(raised)
-        left_buf[...] = jnp.concatenate(
-            [raised_high, raised_low, treated, jnp.zeros_like(treated)], axis=0
-        ).astype(bf16)
-        acc = dot_nn(left_buf[...], high_buf[...]) + dot_nn(left_buf[...], low_buf[...])
-        ux_buf[ux, :, 0:days] = acc[0:groups] + acc[groups:2 * groups]
-        ux_buf[ux, :, days:] = acc[2 * groups:3 * groups]
-        sum_x.start()
-        for k in range(chunks):
+        for k in range(units // CHUNK):
             rows = pl.ds(k * CHUNK, CHUNK)
             high_turned[:, k * CHUNK:(k + 1) * CHUNK] = high_buf[rows, :].T
             low_turned[:, k * CHUNK:(k + 1) * CHUNK] = low_buf[rows, :].T
+        sum_x.wait()
+        uz_buf[uz] = sum_x.total()
+        sum_z.start()
 
     time_rs.wait()
     tzh[dh, 0] = time_rs.total(0, early_ranks)
@@ -279,12 +301,6 @@
     lzh[dh] = lam_rs.total(0, early_ranks)
     lam_zh.start()
 
-    @pl.when(early)
-    def _():
-        sum_x.wait()
-        uz_buf[uz] = sum_x.total()
-        sum_z.start()
-
     stats.wait()
     all_stats = stats.total()
     unit_norm = to_col(all_stats[0:1], groups)
@@ -297,8 +313,8 @@
         sums = sum_z.total()
         residual = (sums[:, 0:days] / unit_norm - sums[:, days:] / treat_count) * before
         res_left = jnp.concatenate(halves(residual), axis=0).astype(bf16)
-        for i in range(shards):
-            cols = slice(i * shard, (i + 1) * shard)
+        for i in range(early_ranks):
+            cols = slice(i * own_units, (i + 1) * own_units)
             out = dot_nn(res_left, high_turned[:, cols]) + dot_nn(res_left, low_turned[:, cols])
             upart[i] = out[0:groups] + out[groups:]
         urs[j] = upart[j]
@@ -311,12 +327,12 @@
     tag[j] = (both[0] / lam_sum - both[1]) * control_buf[j]
     time_ag.start()
 
-    unit_rs.wait()
-    uzh[dh] = unit_rs.total(0, early_ranks)
-    unit_zh.start()
-
-    @pl.when(early)
-    def _():
+    @pl.when(early)
+    def _():
+        unit_rs.wait()
+        uzh[dh] = unit_rs.total()
+        unit_zh.start()
+
         time_ag.wait()
         for i in range(shards):
             left_buf[0:2 * groups, i * shard:(i + 1) * shard] = jnp.concatenate(
@@ -327,15 +343,15 @@
         grad[u] = acc[0:groups] + acc[groups:]
         time_grad.start()
 
-    unit_zh.wait()
-    updated = raised_buf[j] / unit_norm * jnp.exp(-step_rate * unit_zh.total() / jnp.sqrt(before_len))
-    uag[j] = updated
-    utot[u] = to_row(jnp.sum(updated, axis=1, keepdims=True))
-    unit_tot.start()
-    unit_ag.start()
-
-    @pl.when(early)
-    def _():
+    @pl.when(early)
+    def _():
+        unit_zh.wait()
+        updated = raised_buf[j] / unit_norm * jnp.exp(-step_rate * unit_zh.total() / jnp.sqrt(before_len))
+        uag[j] = updated
+        utot[u] = to_row(jnp.sum(updated, axis=1, keepdims=True))
+        unit_tot.start()
+        unit_ag.start()
+
         time_grad.wait()
         ctrl_root = jnp.sqrt(jnp.maximum(ctrl_count, 1.0))
         moved = moved_buf[...] / lam_sum * jnp.exp(-step_rate * time_grad.total() / ctrl_root)
@@ -343,16 +359,16 @@
         ttot[d] = to_row(jnp.sum(moved, axis=1, keepdims=True))
         time_tot.start()
 
-    unit_tot.wait()
-    uall[j] = unit_tot.total()
-    unit_all.start()
+        unit_tot.wait()
+        uall[j] = unit_tot.total()
+        unit_all.start()
 
     unit_ag.wait()
     unit_all.wait()
-    unit_total = jnp.broadcast_to(to_col(unit_all.total(), groups), (groups, shard))
-    count = jnp.broadcast_to(ctrl_count, (groups, shard))
-    for i in range(shards):
-        unit_out[:, i * shard:(i + 1) * shard] = uag[i] / unit_total * count
+    unit_total = jnp.broadcast_to(to_col(unit_all.total(0, early_ranks), groups), (groups, own_units))
+    count = jnp.broadcast_to(ctrl_count, (groups, own_units))
+    for i in range(early_ranks):
+        unit_out[:, i * own_units:(i + 1) * own_units] = uag[i] / unit_total * count
 
     @pl.when(early)
     def _():
@@ -363,12 +379,12 @@
     def _():
         time_out[...] = jnp.zeros_like(time_out)
 
-    for group in (time_rs, stats, time_zh, lam_zh, time_ag, unit_zh, unit_ag, unit_tot, unit_all):
+    for group in (time_rs, stats, time_zh, lam_zh, time_ag):
         group.drain()
 
     @pl.when(early)
     def _():
-        for group in (lam_rs, sum_x, sum_z, unit_rs, time_grad, time_tot):
+        for group in (lam_rs, sum_x, sum_z, unit_rs, unit_zh, unit_tot, unit_ag, unit_all, time_grad, time_tot):
             group.drain()
 
 
@@ -379,6 +395,7 @@
     ny, nh, nc = day_split
     unit_n, day_n, shards = nx * nz, ny * nh * nc, ny * nc
     shard = units // shards
+    own = shards // 2
     hbm = pl.BlockSpec(memory_space=pl.ANY)
     vmem = pl.BlockSpec(memory_space=pltpu.VMEM)
     dma = lambda n: pltpu.SemaphoreType.DMA((n,))
@@ -401,16 +418,17 @@
             pltpu.VMEM((days, units), bf16),
             pltpu.VMEM((days, units), bf16),
             pltpu.VMEM((4 * groups, units), bf16),
-            slots(shards, shard), slots(shards, shard),
+            pltpu.VMEM((4 * groups, days), f32),
+            slots(own, units // own), slots(shards, shard),
             pltpu.VMEM((groups, days), f32),
             slots(unit_n, LANES), slots(nx, 2 * days), slots(nz, 2 * days), slots(unit_n, days),
-            slots(shards, shard), slots(shards, shard), slots(nh, shard), slots(shards, shard),
+            slots(own, units // own), slots(own, units // own), slots(nh, units // own), slots(shards, units // own),
             slots(shards, shard), slots(shards, shard),
             pltpu.VMEM((nh, 2, groups, shard), f32),
             slots(shards, shard),
             rows(shards), rows(nh), rows(unit_n), rows(shards), rows(day_n // 2),
             dma(5),
-            dma(units // CHUNK),
+            dma(PARTS),
             *[dma(2)] * 15,
         ],
         compiler_params=pltpu.CompilerParams(collective_id=0, has_side_effects=True),

time: 40.8 us -> 37.5 us (0.919)
  Pallas kernels: 38.8 us -> 35.5 us
    pallas_call x1, Pallas kernels: 38.8 us -> 35.5 us  [local(): pl.pallas_call(functools.partial(kernel, unit_split, day_split), out_shap...]
where the time goes in v4:
time: 37.5 us; the launch traced here: 37.4 us
  Pallas kernels  35.5 us (95%)
  local copies, waits for them, and re-layouts  1.26 us (3%)
  between operations  0.64 us (2%)
    pallas_call x1, Pallas kernels, local(): pl.pallas_call(functools.partial(kernel, unit_split, day_split), out_shap...  35.5 us
    unnamed x2, local copies, waits for them, and re-layouts  1.26 us

profile of v4, /device:TPU:1, one launch (start us, length us, event | category | flops | bytes accessed | tf_op | source)
XLA Modules:
  0.0 37.4 jit_solution(12052402364556970916)
XLA Ops:
  0.6 35.5 %shard_map.77 = (f32[8,4096]{1,0:T(8,128)S(1)}, f32[8,256]{1,0:T(8,128)S(1)}) custom-call(s32[8]{0:T(128)} %pre_hbm.1, s32[8]{0:T(128)} %post_hbm.1, f32[4096,256]{1,0:T(8,128)} %x_hbm.1, s32[1,4096]{1,0:T(1,128)} %bitcast.1, f32[8,4096]{1,0:T(8,128)} %unit_logit_hbm.1, f32[8,256]{1,0:T(8,128)} %time_logit_hbm.1), custom_call_target="tpu_custom_call" | custom-call | tf_op jit(solution)/shard_map/pallas_call | solution.py:404
  36.2 0.7 %copy.10 = f32[8,4096]{1,0:T(8,128)} copy(f32[8,4096]{1,0:T(8,128)S(1)} %get-tuple-element.2) | data formatting | bytes 262144
  36.8 0.6 %copy.11 = f32[8,256]{1,0:T(8,128)} copy(f32[8,256]{1,0:T(8,128)S(1)} %get-tuple-element.3) | data formatting | bytes 16384

commit v5 on v4

--- a/solution.py
+++ b/solution.py
@@ -103,12 +103,80 @@
         return out
 
 
+class Total:
+    def copy(self, own, place):
+        return pltpu.make_async_remote_copy(
+            src_ref=own, dst_ref=own, send_sem=self.sems.at[0], recv_sem=self.sems.at[1],
+            device_id=place, device_id_type=MESH,
+        )
+
+    def some(self, n):
+        slots = self.buf.at[pl.ds(0, n)]
+        return self.copy(slots, self.any_peer)
+
+    def wait(self):
+        self.some(self.members - 1).wait_recv()
+
+    def total(self):
+        out = self.buf[0]
+        for i in range(1, self.members):
+            out = out + self.buf[i]
+        return out
+
+
+class RingTotal(Total):
+    def __init__(self, buf, sems, ux, uz, nx, nz, steps, on_ring):
+        self.buf, self.sems, self.members = buf, sems, nx * nz
+        self.ux, self.own, self.nx, self.steps, self.on_ring = ux, ux * nz + uz, nx, steps, on_ring
+        self.any_peer = on_ring(ux, 1)
+
+    def start(self):
+        own = self.buf.at[self.own]
+        for step in (0,) + self.steps:
+            for k in range(0 if step else 1, self.nx):
+                self.copy(own, self.on_ring(lax.rem(self.ux + k, self.nx), -step)).start()
+
+    def drain(self):
+        self.some(self.members - 1).wait_send()
+
+
+class DayTotal(Total):
+    def __init__(self, buf, sems, ux, uz, dy, dh, dc, nz, ny, nh, nc, at):
+        self.buf, self.sems, self.members = buf, sems, ny * nh * nc
+        self.ux, self.uz, self.dy, self.dh, self.dc, self.nz, self.ny, self.nh, self.nc, self.at = (
+            ux, uz, dy, dh, dc, nz, ny, nh, nc, at
+        )
+        self.own = dy * (nh * nc) + dh * nc + dc
+        self.rank, self.ranks = dy * nc + dc, ny * nc
+        self.any_peer = at(ux, uz, dy, 1 - dh, dc)
+
+    def start(self):
+        own = self.buf.at[self.own]
+        for k in range(1, self.ranks):
+            peer = lax.rem(self.rank + k, self.ranks)
+            self.copy(own, self.at(self.ux, self.uz, lax.div(peer, self.nc), self.dh, lax.rem(peer, self.nc))).start()
+        for end, firsts in ((self.nz - 1, range(self.nz // 2)), (0, range(self.nz // 2, self.nz))):
+
+            @pl.when(self.uz == end)
+            def _(firsts=firsts):
+                for q in firsts:
+                    for k in range(self.ranks):
+                        self.copy(own, self.at(self.ux, q, k // self.nc, 1 - self.dh, k % self.nc)).start()
+
+    def drain(self):
+        self.some(self.ranks - 1).wait_send()
+
+        @pl.when((self.uz == 0) | (self.uz == self.nz - 1))
+        def _():
+            self.some(self.nz // 2 * self.ranks).wait_send()
+
+
 def kernel(
     unit_split, day_split,
     pre_hbm, post_hbm, x_hbm, cohort_hbm, unit_logit_hbm, time_logit_hbm,
     unit_out, time_out,
     pre_ref, post_ref, cohort_ref, unit_logit_ref, time_logit_ref,
-    x_buf, high_buf, low_buf, high_turned, low_turned, left_buf, acc_buf, raised_buf, control_buf, moved_buf,
+    x_buf, high_buf, low_buf, high_turned, low_turned, left_buf, raised_buf, control_buf, moved_buf,
     stat_buf, ux_buf, uz_buf, grad,
     upart, urs, uzh, uag, tpart, trs, tzh, tag, lrs, lzh, utot, uall, ttot,
     in_sem, x_sem, stat_sem, ux_sem, uz_sem, grad_sem,
@@ -122,7 +190,7 @@
     shard = units // shards
     own_units = units // (shards // 2)
     all_count = day_n * days
-    early_ranks, early_days = shards // 2, day_n // 2
+    early_ranks = shards // 2
 
     u, d = lax.axis_index("unit"), lax.axis_index("day")
     ux, uz = lax.div(u, nz), lax.rem(u, nz)
@@ -136,33 +204,25 @@
     def in_high(rank):
         return {"day": dy * (nh * nc) + rank * nc + dc}
 
+    def at(x, z, y, h, c):
+        return {"unit": x * nz + z, "day": y * (nh * nc) + h * nc + c}
+
+    ring = nh * nz
+    ring_steps = tuple(k for k in range(-(nz // 2) + 1, nz // 2 + 1) if k)
+
+    def on_ring(x, step):
+        z = lax.rem(dh * nz + uz + step + ring, ring)
+        return at(x, lax.rem(z, nz), dy, lax.div(z, nz), dc)
+
     on_unit = lambda rank: {"unit": rank}
-    on_day = lambda rank: {"day": rank}
     on_x = lambda rank: {"unit": rank * nz + uz}
     on_z = lambda rank: {"unit": ux * nz + rank}
-
-    barrier = pltpu.get_barrier_semaphore()
-    for k in range(1, unit_n):
-        pl.semaphore_signal(barrier, inc=1, device_id=on_unit(lax.rem(u + k, unit_n)), device_id_type=MESH)
-    for k in range(1, shards):
-        pl.semaphore_signal(barrier, inc=1, device_id=in_shards(lax.rem(j + k, shards)), device_id_type=MESH)
-    for k in range(1, nh):
-        for i in range(early_ranks):
-            peer = lax.rem(dh + k, nh) * nc + i // nc * nh * nc + i % nc
-
-            @pl.when(early)
-            def _(peer=peer):
-                pl.semaphore_signal(barrier, inc=1, device_id=on_day(peer), device_id_type=MESH)
-
-        @pl.when(jnp.logical_not(early))
-        def _(k=k):
-            pl.semaphore_signal(barrier, inc=1, device_id=in_high(lax.rem(dh + k, nh)), device_id_type=MESH)
 
     inputs = [
         pltpu.make_async_copy(src, dst, in_sem.at[k])
         for k, (src, dst) in enumerate((
-            (unit_logit_hbm, unit_logit_ref), (cohort_hbm, cohort_ref), (time_logit_hbm, time_logit_ref),
-            (pre_hbm, pre_ref), (post_hbm, post_ref),
+            (time_logit_hbm, time_logit_ref), (pre_hbm, pre_ref), (post_hbm, post_ref),
+            (unit_logit_hbm, unit_logit_ref), (cohort_hbm, cohort_ref),
         ))
     ]
     part = units // PARTS
@@ -173,6 +233,32 @@
     for copy in inputs + loads:
         copy.start()
 
+    barrier = pltpu.get_barrier_semaphore()
+
+    def greet(place):
+        pl.semaphore_signal(barrier, inc=1, device_id=place, device_id_type=MESH)
+
+    for k in range(1, unit_n):
+        greet(on_unit(lax.rem(u + k, unit_n)))
+    for k in range(1, shards):
+        greet(in_shards(lax.rem(j + k, shards)))
+
+    @pl.when(early)
+    def _():
+        for k in range(1, nh):
+            for i in range(early_ranks):
+                for q in range(nz):
+                    greet(at(ux, q, i // nc, lax.rem(dh + k, nh), i % nc))
+        for step in ring_steps:
+            for k in range(nx):
+                greet(on_ring(k, step))
+                greet(on_ring(k, -step))
+
+    @pl.when(jnp.logical_not(early))
+    def _():
+        for k in range(1, nh):
+            greet(in_high(lax.rem(dh + k, nh)))
+
     stats = Exchange(stat_buf, stat_sem, u, unit_n, on_unit)
     sum_x = Exchange(ux_buf, ux_sem, ux, nx, on_x)
     sum_z = Exchange(uz_buf, uz_sem, uz, nz, on_z)
@@ -181,7 +267,7 @@
     unit_rs = Exchange(urs, urs_sem, j, early_ranks, in_shards)
     unit_zh = Exchange(uzh, uzh_sem, dh, nh, in_high)
     unit_ag = Exchange(uag, uag_sem, j, shards, in_shards, **from_early)
-    unit_tot = Exchange(utot, utot_sem, u, unit_n, on_unit)
+    unit_tot = RingTotal(utot, utot_sem, ux, uz, nx, nz, ring_steps, on_ring)
     unit_all = Exchange(uall, uall_sem, j, shards, in_shards, **from_early)
     time_rs = Exchange(trs, trs_sem, j, shards, in_shards)
     time_zh = Exchange(tzh, tzh_sem, dh, nh, in_high)
@@ -191,30 +277,10 @@
     lam_rs = Exchange(lrs, lrs_sem, j, shards, in_shards, **from_early)
     lam_zh = Exchange(lzh, lzh_sem, dh, nh, in_high)
     time_grad = Exchange(grad, grad_sem, u, unit_n, on_unit)
-    time_tot = Exchange(ttot, ttot_sem, d, early_days, on_day)
-
-    for copy in inputs:
+    time_tot = DayTotal(ttot, ttot_sem, ux, uz, dy, dh, dc, nz, ny // 2, nh, nc, at)
+
+    for copy in inputs[:3]:
         copy.wait()
-
-    labels = lax.broadcasted_iota(jnp.int32, (groups, units), 0)
-    cohort = jnp.broadcast_to(cohort_ref[...], (groups, units))
-    treated = jnp.where(cohort == labels, 1.0, 0.0)
-    control = jnp.where(cohort > labels, 1.0, 0.0)
-    raised = jnp.exp(unit_logit_ref[...]) * control
-    for i in range(shards):
-        control_buf[i] = control[:, i * shard:(i + 1) * shard]
-    for i in range(early_ranks):
-        raised_buf[i] = raised[:, i * own_units:(i + 1) * own_units]
-    raised_high, raised_low = halves(raised)
-    left_buf[...] = jnp.concatenate(
-        [raised_high, raised_low, treated, jnp.zeros_like(treated)], axis=0
-    ).astype(bf16)
-    norm_part = jnp.sum(raised, axis=1, keepdims=True)
-    treat_part = jnp.sum(treated, axis=1, keepdims=True)
-    ctrl_part = jnp.sum(control, axis=1, keepdims=True)
-    rows3 = [to_row(norm_part), to_row(treat_part), to_row(ctrl_part)]
-    stat_buf[u] = jnp.concatenate(rows3 + [jnp.zeros((groups - 3, LANES), f32)], axis=0)
-
     pre_end, post_start = column(pre_ref, groups), column(post_ref, groups)
     before_len = pre_end.astype(f32)
     after_len = (all_count - post_start).astype(f32)
@@ -240,40 +306,72 @@
             out = dot_nt(time_left, high_buf[rows, :]) + dot_nt(time_left, low_buf[rows, :])
             tpart[i] = (out[0:groups] + out[groups:]) * scale
 
+    def local_weights():
+        for copy in inputs[3:]:
+            copy.wait()
+
+        labels = lax.broadcasted_iota(jnp.int32, (groups, units), 0)
+        cohort = jnp.broadcast_to(cohort_ref[...], (groups, units))
+        treated = jnp.where(cohort == labels, 1.0, 0.0)
+        control = jnp.where(cohort > labels, 1.0, 0.0)
+        raised = jnp.exp(unit_logit_ref[...]) * control
+        for i in range(shards):
+            control_buf[i] = control[:, i * shard:(i + 1) * shard]
+        for i in range(early_ranks):
+            raised_buf[i] = raised[:, i * own_units:(i + 1) * own_units]
+        raised_high, raised_low = halves(raised)
+        left_buf[...] = jnp.concatenate(
+            [raised_high, raised_low, treated, jnp.zeros_like(treated)], axis=0
+        ).astype(bf16)
+        norm_part = jnp.sum(raised, axis=1, keepdims=True)
+        treat_part = jnp.sum(treated, axis=1, keepdims=True)
+        ctrl_part = jnp.sum(control, axis=1, keepdims=True)
+        rows3 = [to_row(norm_part), to_row(treat_part), to_row(ctrl_part)]
+        stat_buf[u] = jnp.concatenate(rows3 + [jnp.zeros((groups - 3, LANES), f32)], axis=0)
+
     def weigh_rows(k):
         rows = pl.ds(k * part, part)
         left = left_buf[:, k * part:(k + 1) * part]
-        return dot_nn(left, high_buf[rows, :]) + dot_nn(left, low_buf[rows, :])
-
-    for k in range(PARTS):
-        loads[k].wait()
-        split(k)
-
-        @pl.when(early)
-        def _(k=k):
-            acc = weigh_rows(k)
+        acc = dot_nn(left, high_buf[rows, :]) + dot_nn(left, low_buf[rows, :])
+        fit, treat = acc[0:groups] + acc[groups:2 * groups], acc[2 * groups:3 * groups]
+        if k:
+            fit, treat = fit + own_sums[:, 0:days], treat + own_sums[:, days:]
+        own_sums[:, 0:days] = fit
+        own_sums[:, days:] = treat
+
+    own_sums = ux_buf.at[ux]
+
+    @pl.when(early)
+    def _():
+        local_weights()
+        for k in range(PARTS):
+            loads[k].wait()
             if k:
-                acc_buf[...] += acc
-            else:
-                acc_buf[...] = acc
-
-    @pl.when(early)
-    def _():
-        ux_buf[ux, :, 0:days] = acc_buf[0:groups] + acc_buf[groups:2 * groups]
-        ux_buf[ux, :, days:] = acc_buf[2 * groups:3 * groups]
-
-    for k in range(PARTS // 2):
-        weigh_units(k)
+                weigh_rows(k - 1)
+            split(k)
+        weigh_rows(PARTS - 1)
+        weigh_units(0)
+
+    @pl.when(jnp.logical_not(early))
+    def _():
+        for k in range(PARTS):
+            loads[k].wait()
+            if k:
+                weigh_units(k - 1)
+            split(k)
+        weigh_units(PARTS - 1)
 
     pl.semaphore_wait(
-        barrier, unit_n - 1 + shards - 1 + jnp.where(early, (nh - 1) * early_ranks, nh - 1)
+        barrier,
+        unit_n - 1 + shards - 1
+        + jnp.where(early, (nh - 1) * early_ranks * nz + 2 * len(ring_steps) * nx, nh - 1),
     )
     @pl.when(early)
     def _():
         sum_x.start()
-
-    for k in range(PARTS // 2, PARTS):
-        weigh_units(k)
+        for k in range(1, PARTS):
+            weigh_units(k)
+
     trs[j] = tpart[j]
     time_rs.start(tpart)
 
@@ -281,6 +379,7 @@
     def _():
         lam_rs.start()
 
+    pl.when(jnp.logical_not(early))(local_weights)
     stats.start()
 
     @pl.when(early)
@@ -289,6 +388,9 @@
             rows = pl.ds(k * CHUNK, CHUNK)
             high_turned[:, k * CHUNK:(k + 1) * CHUNK] = high_buf[rows, :].T
             low_turned[:, k * CHUNK:(k + 1) * CHUNK] = low_buf[rows, :].T
+
+    @pl.when(early)
+    def _():
         sum_x.wait()
         uz_buf[uz] = sum_x.total()
         sum_z.start()
@@ -386,6 +488,17 @@
     def _():
         for group in (lam_rs, sum_x, sum_z, unit_rs, unit_zh, unit_tot, unit_ag, unit_all, time_grad, time_tot):
             group.drain()
+
+
+def put_out(unit_in, time_in, unit_out, time_out, sems):
+    copies = [
+        pltpu.make_async_copy(unit_in, unit_out, sems.at[0]),
+        pltpu.make_async_copy(time_in, time_out, sems.at[1]),
+    ]
+    for copy in copies:
+        copy.start()
+    for copy in copies:
+        copy.wait()
 
 
 def local(unit_split, day_split, outcomes, cohort, pre_end, post_start, unit_logit, time_logit):
@@ -401,7 +514,7 @@
     dma = lambda n: pltpu.SemaphoreType.DMA((n,))
     slots = lambda n, size: pltpu.VMEM((n, groups, size), f32)
     rows = lambda n: pltpu.VMEM((n, 1, LANES), f32)
-    return pl.pallas_call(
+    unit_weights, time_weights = pl.pallas_call(
         functools.partial(kernel, unit_split, day_split),
         out_shape=(pltpu.VMEM((groups, units), f32), pltpu.VMEM((groups, days), f32)),
         in_specs=[hbm] * 6,
@@ -418,7 +531,6 @@
             pltpu.VMEM((days, units), bf16),
             pltpu.VMEM((days, units), bf16),
             pltpu.VMEM((4 * groups, units), bf16),
-            pltpu.VMEM((4 * groups, days), f32),
             slots(own, units // own), slots(shards, shard),
             pltpu.VMEM((groups, days), f32),
             slots(unit_n, LANES), slots(nx, 2 * days), slots(nz, 2 * days), slots(unit_n, days),
@@ -433,6 +545,16 @@
         ],
         compiler_params=pltpu.CompilerParams(collective_id=0, has_side_effects=True),
     )(pre_end, post_start, outcomes, cohort.reshape(1, units), unit_logit, time_logit)
+    return pl.pallas_call(
+        put_out,
+        out_shape=(
+            jax.ShapeDtypeStruct((groups, units), f32),
+            jax.ShapeDtypeStruct((groups, days), f32),
+        ),
+        in_specs=[vmem] * 2,
+        out_specs=(hbm, hbm),
+        scratch_shapes=[dma(2)],
+    )(*(pltpu.with_memory_space_constraint(v, pltpu.VMEM) for v in (unit_weights, time_weights)))
 
 
 def solution(mesh):

time: 37.5 us -> 36.4 us (0.971)
  local copies, waits for them, and re-layouts: 1.26 us -> 0 us
    unnamed x2 -> x0, local copies, waits for them, and re-layouts: 1.26 us -> none
    pallas_call x0 -> x1, Pallas kernels: none -> 0.68 us  [local(): pl.pallas_call(put_out, out_shape=(jax.ShapeDtypeStruct((groups, units),...]
    pallas_call x1, Pallas kernels: 35.5 us -> 35 us  [local(): pl.pallas_call(functools.partial(kernel, unit_split, day_split), out_shap...]
where the time goes in v5:
time: 36.4 us; the launch traced here: 36.3 us
  Pallas kernels  35.6 us (98%)
  between operations  0.64 us (2%)
    pallas_call x1, Pallas kernels, local(): pl.pallas_call(functools.partial(kernel, unit_split, day_split), out_shap...  35 us

profile of v5, /device:TPU:1, one launch (start us, length us, event | category | flops | bytes accessed | tf_op | source)
XLA Modules:
  0.0 36.3 jit_solution(13738204030080777725)
XLA Ops:
  0.6 35.0 %shard_map.77 = (f32[8,4096]{1,0:T(8,128)S(1)}, f32[8,256]{1,0:T(8,128)S(1)}) custom-call(s32[8]{0:T(128)} %pre_hbm.1, s32[8]{0:T(128)} %post_hbm.1, f32[4096,256]{1,0:T(8,128)} %x_hbm.1, s32[1,4096]{1,0:T(1,128)} %bitcast.1, f32[8,4096]{1,0:T(8,128)} %unit_logit_hbm.1, f32[8,256]{1,0:T(8,128)} %time_logit_hbm.1), custom_call_target="tpu_custom_call" | custom-call | tf_op jit(solution)/shard_map/pallas_call | solution.py:517
  35.6 0.7 %shard_map.78 = (f32[8,4096]{1,0:T(8,128)}, f32[8,256]{1,0:T(8,128)}) custom-call(f32[8,4096]{1,0:T(8,128)S(1)} %get-tuple-element.4.unit_in, f32[8,256]{1,0:T(8,128)S(1)} %get-tuple-element.5.time_in), custom_call_target="tpu_custom_call" | custom-call | tf_op jit(solution)/shard_map/pallas_call | solution.py:548

commit v6 on v5

--- a/solution.py
+++ b/solution.py
@@ -30,17 +30,17 @@
     return high, v - high
 
 
-def to_row(col):
+def to_row(col, first=0):
     groups = col.shape[0]
     row_id = lax.broadcasted_iota(jnp.int32, (groups, LANES), 0)
     lane_id = lax.broadcasted_iota(jnp.int32, (groups, LANES), 1)
-    return jnp.sum(jnp.where(row_id == lane_id, col, 0.0), axis=0, keepdims=True)
-
-
-def to_col(row, groups):
+    return jnp.sum(jnp.where(row_id + first == lane_id, col, 0.0), axis=0, keepdims=True)
+
+
+def to_col(row, groups, first=0):
     row_id = lax.broadcasted_iota(jnp.int32, (groups, LANES), 0)
     lane_id = lax.broadcasted_iota(jnp.int32, (groups, LANES), 1)
-    return jnp.sum(jnp.where(row_id == lane_id, row, 0.0), axis=1, keepdims=True)
+    return jnp.sum(jnp.where(row_id + first == lane_id, row, 0.0), axis=1, keepdims=True)
 
 
 def column(ref, groups):
@@ -179,7 +179,7 @@
     x_buf, high_buf, low_buf, high_turned, low_turned, left_buf, raised_buf, control_buf, moved_buf,
     stat_buf, ux_buf, uz_buf, grad,
     upart, urs, uzh, uag, tpart, trs, tzh, tag, lrs, lzh, utot, uall, ttot,
-    in_sem, x_sem, stat_sem, ux_sem, uz_sem, grad_sem,
+    in_sem, x_sem, near_sem, ux_sem, uz_sem, grad_sem,
     urs_sem, uzh_sem, uag_sem, trs_sem, tzh_sem, tag_sem, lrs_sem, lzh_sem, utot_sem, uall_sem, ttot_sem,
 ):
     nx, nz = unit_split
@@ -217,6 +217,21 @@
     on_unit = lambda rank: {"unit": rank}
     on_x = lambda rank: {"unit": rank * nz + uz}
     on_z = lambda rank: {"unit": ux * nz + rank}
+
+    barrier = pltpu.get_barrier_semaphore()
+
+    def greet(place):
+        pl.semaphore_signal(barrier, inc=1, device_id=place, device_id_type=MESH)
+
+    for k in range(1, shards):
+        greet(in_shards(lax.rem(j + k, shards)))
+    for step in (-2, -1, 1, 2):
+        greet(on_ring(ux, step))
+
+    @pl.when(early)
+    def _():
+        for k in range(1, nx):
+            greet(on_x(lax.rem(ux + k, nx)))
 
     inputs = [
         pltpu.make_async_copy(src, dst, in_sem.at[k])
@@ -233,33 +248,6 @@
     for copy in inputs + loads:
         copy.start()
 
-    barrier = pltpu.get_barrier_semaphore()
-
-    def greet(place):
-        pl.semaphore_signal(barrier, inc=1, device_id=place, device_id_type=MESH)
-
-    for k in range(1, unit_n):
-        greet(on_unit(lax.rem(u + k, unit_n)))
-    for k in range(1, shards):
-        greet(in_shards(lax.rem(j + k, shards)))
-
-    @pl.when(early)
-    def _():
-        for k in range(1, nh):
-            for i in range(early_ranks):
-                for q in range(nz):
-                    greet(at(ux, q, i // nc, lax.rem(dh + k, nh), i % nc))
-        for step in ring_steps:
-            for k in range(nx):
-                greet(on_ring(k, step))
-                greet(on_ring(k, -step))
-
-    @pl.when(jnp.logical_not(early))
-    def _():
-        for k in range(1, nh):
-            greet(in_high(lax.rem(dh + k, nh)))
-
-    stats = Exchange(stat_buf, stat_sem, u, unit_n, on_unit)
     sum_x = Exchange(ux_buf, ux_sem, ux, nx, on_x)
     sum_z = Exchange(uz_buf, uz_sem, uz, nz, on_z)
     to_early = (early_ranks - 1, early_ranks)
@@ -293,6 +281,10 @@
     scale = jnp.broadcast_to(jnp.where(early, 1.0, 1.0 / after_len), (groups, shard))
     lrs[j] = to_row(jnp.sum(time_raised, axis=1, keepdims=True))
 
+    def hear():
+        pl.semaphore_wait(near_sem.at[0], 1)
+        pl.semaphore_wait(near_sem.at[1], 1)
+
     def split(k):
         rows = pl.ds(k * part, part)
         whole = x_buf[rows, :]
@@ -326,8 +318,10 @@
         norm_part = jnp.sum(raised, axis=1, keepdims=True)
         treat_part = jnp.sum(treated, axis=1, keepdims=True)
         ctrl_part = jnp.sum(control, axis=1, keepdims=True)
-        rows3 = [to_row(norm_part), to_row(treat_part), to_row(ctrl_part)]
-        stat_buf[u] = jnp.concatenate(rows3 + [jnp.zeros((groups - 3, LANES), f32)], axis=0)
+        lane = lax.broadcasted_iota(jnp.int32, (groups, LANES), 1)
+        ux_buf[ux, :, 2 * days:] = jnp.where(
+            lane == 0, norm_part, jnp.where(lane == 1, treat_part, jnp.where(lane == 2, ctrl_part, 0.0))
+        )
 
     def weigh_rows(k):
         rows = pl.ds(k * part, part)
@@ -335,11 +329,22 @@
         acc = dot_nn(left, high_buf[rows, :]) + dot_nn(left, low_buf[rows, :])
         fit, treat = acc[0:groups] + acc[groups:2 * groups], acc[2 * groups:3 * groups]
         if k:
-            fit, treat = fit + own_sums[:, 0:days], treat + own_sums[:, days:]
+            fit, treat = fit + own_sums[:, 0:days], treat + own_sums[:, days:2 * days]
         own_sums[:, 0:days] = fit
-        own_sums[:, days:] = treat
+        own_sums[:, days:2 * days] = treat
 
     own_sums = ux_buf.at[ux]
+
+    def turn(k):
+        for i in range(k * part // CHUNK, (k + 1) * part // CHUNK):
+            rows = pl.ds(i * CHUNK, CHUNK)
+            high_turned[:, i * CHUNK:(i + 1) * CHUNK] = high_buf[rows, :].T
+            low_turned[:, i * CHUNK:(i + 1) * CHUNK] = low_buf[rows, :].T
+
+    def weigh_turned(i):
+        cols = slice(i * shard, (i + 1) * shard)
+        out = dot_nn(time_left, high_turned[:, cols]) + dot_nn(time_left, low_turned[:, cols])
+        tpart[i] = (out[0:groups] + out[groups:]) * scale
 
     @pl.when(early)
     def _():
@@ -347,10 +352,13 @@
         for k in range(PARTS):
             loads[k].wait()
             if k:
+                turn(k - 1)
                 weigh_rows(k - 1)
             split(k)
+        turn(PARTS - 1)
         weigh_rows(PARTS - 1)
-        weigh_units(0)
+        for i in range(shards // 2):
+            weigh_turned(i)
 
     @pl.when(jnp.logical_not(early))
     def _():
@@ -361,16 +369,15 @@
             split(k)
         weigh_units(PARTS - 1)
 
-    pl.semaphore_wait(
-        barrier,
-        unit_n - 1 + shards - 1
-        + jnp.where(early, (nh - 1) * early_ranks * nz + 2 * len(ring_steps) * nx, nh - 1),
-    )
+    pl.semaphore_wait(barrier, shards - 1 + 4 + jnp.where(early, nx - 1, 0))
+    pl.semaphore_signal(near_sem.at[0], inc=1, device_id=on_ring(ux, 2), device_id_type=MESH)
+    pl.semaphore_signal(near_sem.at[1], inc=1, device_id=on_ring(ux, -2), device_id_type=MESH)
+
     @pl.when(early)
     def _():
         sum_x.start()
-        for k in range(1, PARTS):
-            weigh_units(k)
+        for i in range(shards // 2, shards):
+            weigh_turned(i)
 
     trs[j] = tpart[j]
     time_rs.start(tpart)
@@ -380,20 +387,16 @@
         lam_rs.start()
 
     pl.when(jnp.logical_not(early))(local_weights)
-    stats.start()
-
-    @pl.when(early)
-    def _():
-        for k in range(units // CHUNK):
-            rows = pl.ds(k * CHUNK, CHUNK)
-            high_turned[:, k * CHUNK:(k + 1) * CHUNK] = high_buf[rows, :].T
-            low_turned[:, k * CHUNK:(k + 1) * CHUNK] = low_buf[rows, :].T
-
     @pl.when(early)
     def _():
         sum_x.wait()
         uz_buf[uz] = sum_x.total()
+        hear()
         sum_z.start()
+
+    @pl.when(jnp.logical_not(early))
+    def _():
+        hear()
 
     time_rs.wait()
     tzh[dh, 0] = time_rs.total(0, early_ranks)
@@ -403,17 +406,14 @@
     lzh[dh] = lam_rs.total(0, early_ranks)
     lam_zh.start()
 
-    stats.wait()
-    all_stats = stats.total()
-    unit_norm = to_col(all_stats[0:1], groups)
-    treat_count = jnp.maximum(to_col(all_stats[1:2], groups), 1.0)
-    ctrl_count = to_col(all_stats[2:3], groups)
-
     @pl.when(early)
     def _():
         sum_z.wait()
         sums = sum_z.total()
-        residual = (sums[:, 0:days] / unit_norm - sums[:, days:] / treat_count) * before
+        stat_buf[...] = sums[:, 2 * days:]
+        unit_norm = sums[:, 2 * days:2 * days + 1]
+        treat_count = jnp.maximum(sums[:, 2 * days + 1:2 * days + 2], 1.0)
+        residual = (sums[:, 0:days] / unit_norm - sums[:, days:2 * days] / treat_count) * before
         res_left = jnp.concatenate(halves(residual), axis=0).astype(bf16)
         for i in range(early_ranks):
             cols = slice(i * own_units, (i + 1) * own_units)
@@ -448,27 +448,27 @@
     @pl.when(early)
     def _():
         unit_zh.wait()
-        updated = raised_buf[j] / unit_norm * jnp.exp(-step_rate * unit_zh.total() / jnp.sqrt(before_len))
+        updated = raised_buf[j] / stat_buf[:, 0:1] * jnp.exp(-step_rate * unit_zh.total() / jnp.sqrt(before_len))
         uag[j] = updated
         utot[u] = to_row(jnp.sum(updated, axis=1, keepdims=True))
         unit_tot.start()
         unit_ag.start()
 
         time_grad.wait()
-        ctrl_root = jnp.sqrt(jnp.maximum(ctrl_count, 1.0))
+        ctrl_root = jnp.sqrt(jnp.maximum(stat_buf[:, 2:3], 1.0))
         moved = moved_buf[...] / lam_sum * jnp.exp(-step_rate * time_grad.total() / ctrl_root)
         moved_buf[...] = moved
         ttot[d] = to_row(jnp.sum(moved, axis=1, keepdims=True))
         time_tot.start()
 
         unit_tot.wait()
-        uall[j] = unit_tot.total()
+        uall[j] = unit_tot.total() + to_row(stat_buf[:, 2:3], groups)
         unit_all.start()
 
     unit_ag.wait()
     unit_all.wait()
     unit_total = jnp.broadcast_to(to_col(unit_all.total(0, early_ranks), groups), (groups, own_units))
-    count = jnp.broadcast_to(ctrl_count, (groups, own_units))
+    count = jnp.broadcast_to(to_col(uall[0], groups, groups), (groups, own_units))
     for i in range(early_ranks):
         unit_out[:, i * own_units:(i + 1) * own_units] = uag[i] / unit_total * count
 
@@ -481,7 +481,7 @@
     def _():
         time_out[...] = jnp.zeros_like(time_out)
 
-    for group in (time_rs, stats, time_zh, lam_zh, time_ag):
+    for group in (time_rs, time_zh, lam_zh, time_ag):
         group.drain()
 
     @pl.when(early)
@@ -533,7 +533,8 @@
             pltpu.VMEM((4 * groups, units), bf16),
             slots(own, units // own), slots(shards, shard),
             pltpu.VMEM((groups, days), f32),
-            slots(unit_n, LANES), slots(nx, 2 * days), slots(nz, 2 * days), slots(unit_n, days),
+            pltpu.VMEM((groups, LANES), f32),
+            slots(nx, 2 * days + LANES), slots(nz, 2 * days + LANES), slots(unit_n, days),
             slots(own, units // own), slots(own, units // own), slots(nh, units // own), slots(shards, units // own),
             slots(shards, shard), slots(shards, shard),
             pltpu.VMEM((nh, 2, groups, shard), f32),
@@ -541,7 +542,8 @@
             rows(shards), rows(nh), rows(unit_n), rows(shards), rows(day_n // 2),
             dma(5),
             dma(PARTS),
-            *[dma(2)] * 15,
+            pltpu.SemaphoreType.REGULAR((2,)),
+            *[dma(2)] * 14,
         ],
         compiler_params=pltpu.CompilerParams(collective_id=0, has_side_effects=True),
     )(pre_end, post_start, outcomes, cohort.reshape(1, units), unit_logit, time_logit)

time: 36.4 us -> 35.7 us (0.981)
  Pallas kernels: 35.6 us -> 35 us
    pallas_call x1, Pallas kernels: 35 us -> 34.3 us  [local(): pl.pallas_call(functools.partial(kernel, unit_split, day_split), out_shap...]
where the time goes in v6:
time: 35.7 us; the launch traced here: 35.6 us
  Pallas kernels  35 us (98%)
  between operations  0.64 us (2%)
    pallas_call x1, Pallas kernels, local(): pl.pallas_call(functools.partial(kernel, unit_split, day_split), out_shap...  34.3 us

profile of v6, /device:TPU:1, one launch (start us, length us, event | category | flops | bytes accessed | tf_op | source)
XLA Modules:
  0.0 35.6 jit_solution(13980978154414631333)
XLA Ops:
  0.6 34.3 %shard_map.77 = (f32[8,4096]{1,0:T(8,128)S(1)}, f32[8,256]{1,0:T(8,128)S(1)}) custom-call(s32[8]{0:T(128)} %pre_hbm.1, s32[8]{0:T(128)} %post_hbm.1, f32[4096,256]{1,0:T(8,128)} %x_hbm.1, s32[1,4096]{1,0:T(1,128)} %bitcast.1, f32[8,4096]{1,0:T(8,128)} %unit_logit_hbm.1, f32[8,256]{1,0:T(8,128)} %time_logit_hbm.1), custom_call_target="tpu_custom_call" | custom-call | tf_op jit(solution)/shard_map/pallas_call | solution.py:517
  34.9 0.7 %shard_map.78 = (f32[8,4096]{1,0:T(8,128)}, f32[8,256]{1,0:T(8,128)}) custom-call(f32[8,4096]{1,0:T(8,128)S(1)} %get-tuple-element.4.unit_in, f32[8,256]{1,0:T(8,128)S(1)} %get-tuple-element.5.time_in), custom_call_target="tpu_custom_call" | custom-call | tf_op jit(solution)/shard_map/pallas_call | solution.py:550

commit v7 on v6

--- a/solution.py
+++ b/solution.py
@@ -125,19 +125,47 @@
 
 
 class RingTotal(Total):
-    def __init__(self, buf, sems, ux, uz, nx, nz, steps, on_ring):
-        self.buf, self.sems, self.members = buf, sems, nx * nz
-        self.ux, self.own, self.nx, self.steps, self.on_ring = ux, ux * nz + uz, nx, steps, on_ring
+    def __init__(self, buf, sems, ux, uz, dy, nx, nz, ny, steps, on_ring):
+        self.buf, self.sems, self.members = buf, sems, nx * nz * ny
+        self.ux, self.dy, self.own = ux, dy, (ux * nz + uz) * ny + dy
+        self.nx, self.ny, self.steps, self.on_ring = nx, ny, steps, on_ring
         self.any_peer = on_ring(ux, 1)
 
     def start(self):
         own = self.buf.at[self.own]
         for step in (0,) + self.steps:
-            for k in range(0 if step else 1, self.nx):
-                self.copy(own, self.on_ring(lax.rem(self.ux + k, self.nx), -step)).start()
+            for k in range(self.nx):
+                for i in range(self.ny):
+                    if step or k or i:
+                        x, y = lax.rem(self.ux + k, self.nx), lax.rem(self.dy + i, self.ny)
+                        self.copy(own, self.on_ring(x, -step, y)).start()
 
     def drain(self):
         self.some(self.members - 1).wait_send()
+
+
+class CoreTotal(Total):
+    def __init__(self, buf, sems, ux, uz, dy, dh, dc, ny, nc, flag, at):
+        self.buf, self.sems, self.members, self.flag = buf, sems, nc, flag
+        self.dc, self.nc = dc, nc
+        self.beside = lambda c: at(ux, uz, dy, dh, c)
+        self.across = lambda c: at(ux, uz, ny - 1 - dy, dh, c)
+        self.any_peer = self.across(dc)
+
+    def start(self):
+        own = self.buf.at[self.dc]
+        for k in range(1, self.nc):
+            self.copy(own, self.beside(lax.rem(self.dc + k, self.nc))).start()
+        for c in range(self.nc):
+            self.copy(own, self.across(c)).start()
+
+    def wait(self):
+        if self.nc > 1:
+            pl.when(self.flag)(lambda: self.some(self.nc - 1).wait_recv())
+        pl.when(jnp.logical_not(self.flag))(lambda: self.some(self.nc).wait_recv())
+
+    def drain(self):
+        self.some(2 * self.nc - 1).wait_send()
 
 
 class DayTotal(Total):
@@ -210,9 +238,9 @@
     ring = nh * nz
     ring_steps = tuple(k for k in range(-(nz // 2) + 1, nz // 2 + 1) if k)
 
-    def on_ring(x, step):
+    def on_ring(x, step, y=None):
         z = lax.rem(dh * nz + uz + step + ring, ring)
-        return at(x, lax.rem(z, nz), dy, lax.div(z, nz), dc)
+        return at(x, lax.rem(z, nz), dy if y is None else y, lax.div(z, nz), dc)
 
     on_unit = lambda rank: {"unit": rank}
     on_x = lambda rank: {"unit": rank * nz + uz}
@@ -255,8 +283,8 @@
     unit_rs = Exchange(urs, urs_sem, j, early_ranks, in_shards)
     unit_zh = Exchange(uzh, uzh_sem, dh, nh, in_high)
     unit_ag = Exchange(uag, uag_sem, j, shards, in_shards, **from_early)
-    unit_tot = RingTotal(utot, utot_sem, ux, uz, nx, nz, ring_steps, on_ring)
-    unit_all = Exchange(uall, uall_sem, j, shards, in_shards, **from_early)
+    unit_tot = RingTotal(utot, utot_sem, ux, uz, dy, nx, nz, ny // 2, ring_steps, on_ring)
+    unit_all = CoreTotal(uall, uall_sem, ux, uz, dy, dh, dc, ny, nc, early, at)
     time_rs = Exchange(trs, trs_sem, j, shards, in_shards)
     time_zh = Exchange(tzh, tzh_sem, dh, nh, in_high)
     time_ag = Exchange(
@@ -323,68 +351,33 @@
             lane == 0, norm_part, jnp.where(lane == 1, treat_part, jnp.where(lane == 2, ctrl_part, 0.0))
         )
 
-    def weigh_rows(k):
-        rows = pl.ds(k * part, part)
-        left = left_buf[:, k * part:(k + 1) * part]
-        acc = dot_nn(left, high_buf[rows, :]) + dot_nn(left, low_buf[rows, :])
-        fit, treat = acc[0:groups] + acc[groups:2 * groups], acc[2 * groups:3 * groups]
+    for k in range(PARTS):
+        loads[k].wait()
         if k:
-            fit, treat = fit + own_sums[:, 0:days], treat + own_sums[:, days:2 * days]
-        own_sums[:, 0:days] = fit
-        own_sums[:, days:2 * days] = treat
-
-    own_sums = ux_buf.at[ux]
-
-    def turn(k):
-        for i in range(k * part // CHUNK, (k + 1) * part // CHUNK):
-            rows = pl.ds(i * CHUNK, CHUNK)
-            high_turned[:, i * CHUNK:(i + 1) * CHUNK] = high_buf[rows, :].T
-            low_turned[:, i * CHUNK:(i + 1) * CHUNK] = low_buf[rows, :].T
-
-    def weigh_turned(i):
-        cols = slice(i * shard, (i + 1) * shard)
-        out = dot_nn(time_left, high_turned[:, cols]) + dot_nn(time_left, low_turned[:, cols])
-        tpart[i] = (out[0:groups] + out[groups:]) * scale
-
-    @pl.when(early)
-    def _():
-        local_weights()
-        for k in range(PARTS):
-            loads[k].wait()
-            if k:
-                turn(k - 1)
-                weigh_rows(k - 1)
-            split(k)
-        turn(PARTS - 1)
-        weigh_rows(PARTS - 1)
-        for i in range(shards // 2):
-            weigh_turned(i)
-
-    @pl.when(jnp.logical_not(early))
-    def _():
-        for k in range(PARTS):
-            loads[k].wait()
-            if k:
-                weigh_units(k - 1)
-            split(k)
-        weigh_units(PARTS - 1)
+            weigh_units(k - 1)
+        split(k)
+        if k == 2:
+            pl.when(early)(local_weights)
+    weigh_units(PARTS - 1)
+    trs[j] = tpart[j]
 
     pl.semaphore_wait(barrier, shards - 1 + 4 + jnp.where(early, nx - 1, 0))
     pl.semaphore_signal(near_sem.at[0], inc=1, device_id=on_ring(ux, 2), device_id_type=MESH)
     pl.semaphore_signal(near_sem.at[1], inc=1, device_id=on_ring(ux, -2), device_id_type=MESH)
 
-    @pl.when(early)
-    def _():
+    time_rs.start(tpart)
+
+    @pl.when(early)
+    def _():
+        lam_rs.start()
+        acc = dot_nn(left_buf[...], high_buf[...]) + dot_nn(left_buf[...], low_buf[...])
+        ux_buf[ux, :, 0:days] = acc[0:groups] + acc[groups:2 * groups]
+        ux_buf[ux, :, days:2 * days] = acc[2 * groups:3 * groups]
         sum_x.start()
-        for i in range(shards // 2, shards):
-            weigh_turned(i)
-
-    trs[j] = tpart[j]
-    time_rs.start(tpart)
-
-    @pl.when(early)
-    def _():
-        lam_rs.start()
+        for k in range(units // CHUNK):
+            rows = pl.ds(k * CHUNK, CHUNK)
+            high_turned[:, k * CHUNK:(k + 1) * CHUNK] = high_buf[rows, :].T
+            low_turned[:, k * CHUNK:(k + 1) * CHUNK] = low_buf[rows, :].T
 
     pl.when(jnp.logical_not(early))(local_weights)
     @pl.when(early)
@@ -450,7 +443,7 @@
         unit_zh.wait()
         updated = raised_buf[j] / stat_buf[:, 0:1] * jnp.exp(-step_rate * unit_zh.total() / jnp.sqrt(before_len))
         uag[j] = updated
-        utot[u] = to_row(jnp.sum(updated, axis=1, keepdims=True))
+        utot[unit_tot.own] = to_row(jnp.sum(updated, axis=1, keepdims=True))
         unit_tot.start()
         unit_ag.start()
 
@@ -462,12 +455,12 @@
         time_tot.start()
 
         unit_tot.wait()
-        uall[j] = unit_tot.total() + to_row(stat_buf[:, 2:3], groups)
+        uall[dc] = unit_tot.total() + to_row(stat_buf[:, 2:3], groups)
         unit_all.start()
 
     unit_ag.wait()
     unit_all.wait()
-    unit_total = jnp.broadcast_to(to_col(unit_all.total(0, early_ranks), groups), (groups, own_units))
+    unit_total = jnp.broadcast_to(to_col(unit_all.total(), groups), (groups, own_units))
     count = jnp.broadcast_to(to_col(uall[0], groups, groups), (groups, own_units))
     for i in range(early_ranks):
         unit_out[:, i * own_units:(i + 1) * own_units] = uag[i] / unit_total * count
@@ -539,7 +532,7 @@
             slots(shards, shard), slots(shards, shard),
             pltpu.VMEM((nh, 2, groups, shard), f32),
             slots(shards, shard),
-            rows(shards), rows(nh), rows(unit_n), rows(shards), rows(day_n // 2),
+            rows(shards), rows(nh), rows(unit_n * ny // 2), rows(2 * nc), rows(day_n // 2),
             dma(5),
             dma(PARTS),
             pltpu.SemaphoreType.REGULAR((2,)),

time: 35.7 us -> 35.7 us (level)
  no operation moved by 1% of the time
where the time goes in v7:
time: 35.7 us; the launch traced here: 35.6 us
  Pallas kernels  35 us (98%)
  between operations  0.64 us (2%)
    pallas_call x1, Pallas kernels, local(): pl.pallas_call(functools.partial(kernel, unit_split, day_split), out_shap...  34.3 us

profile of v7, /device:TPU:1, one launch (start us, length us, event | category | flops | bytes accessed | tf_op | source)
XLA Modules:
  0.0 35.6 jit_solution(6493903256175578399)
XLA Ops:
  0.6 34.3 %shard_map.77 = (f32[8,4096]{1,0:T(8,128)S(1)}, f32[8,256]{1,0:T(8,128)S(1)}) custom-call(s32[8]{0:T(128)} %pre_hbm.1, s32[8]{0:T(128)} %post_hbm.1, f32[4096,256]{1,0:T(8,128)} %x_hbm.1, s32[1,4096]{1,0:T(1,128)} %bitcast.1, f32[8,4096]{1,0:T(8,128)} %unit_logit_hbm.1, f32[8,256]{1,0:T(8,128)} %time_logit_hbm.1), custom_call_target="tpu_custom_call" | custom-call | tf_op jit(solution)/shard_map/pallas_call | solution.py:510
  34.9 0.7 %shard_map.78 = (f32[8,4096]{1,0:T(8,128)}, f32[8,256]{1,0:T(8,128)}) custom-call(f32[8,4096]{1,0:T(8,128)S(1)} %get-tuple-element.4.unit_in, f32[8,256]{1,0:T(8,128)S(1)} %get-tuple-element.5.time_in), custom_call_target="tpu_custom_call" | custom-call | tf_op jit(solution)/shard_map/pallas_call | solution.py:543

commit v8 on v7

--- a/solution.py
+++ b/solution.py
@@ -434,7 +434,10 @@
                 halves(tag[i]), axis=0
             ).astype(bf16)
         left = left_buf[0:2 * groups, :]
-        acc = dot_nn(left, high_buf[...]) + dot_nn(left, low_buf[...])
+        mid = units // 2
+        acc = (dot_nn(left[:, :mid], high_buf[:mid, :]) + dot_nn(left[:, :mid], low_buf[:mid, :])) + (
+            dot_nn(left[:, mid:], high_buf[mid:, :]) + dot_nn(left[:, mid:], low_buf[mid:, :])
+        )
         grad[u] = acc[0:groups] + acc[groups:]
         time_grad.start()
 

time: 35.7 us -> 35.7 us (level)
  no operation moved by 1% of the time
where the time goes in v8:
time: 35.7 us; the launch traced here: 35.6 us
  Pallas kernels  35 us (98%)
  between operations  0.64 us (2%)
    pallas_call x1, Pallas kernels, local(): pl.pallas_call(functools.partial(kernel, unit_split, day_split), out_shap...  34.3 us

profile of v8, /device:TPU:1, one launch (start us, length us, event | category | flops | bytes accessed | tf_op | source)
XLA Modules:
  0.0 35.6 jit_solution(2122259849958141742)
XLA Ops:
  0.6 34.3 %shard_map.77 = (f32[8,4096]{1,0:T(8,128)S(1)}, f32[8,256]{1,0:T(8,128)S(1)}) custom-call(s32[8]{0:T(128)} %pre_hbm.1, s32[8]{0:T(128)} %post_hbm.1, f32[4096,256]{1,0:T(8,128)} %x_hbm.1, s32[1,4096]{1,0:T(1,128)} %bitcast.1, f32[8,4096]{1,0:T(8,128)} %unit_logit_hbm.1, f32[8,256]{1,0:T(8,128)} %time_logit_hbm.1), custom_call_target="tpu_custom_call" | custom-call | tf_op jit(solution)/shard_map/pallas_call | solution.py:513
  34.9 0.7 %shard_map.78 = (f32[8,4096]{1,0:T(8,128)}, f32[8,256]{1,0:T(8,128)}) custom-call(f32[8,4096]{1,0:T(8,128)S(1)} %get-tuple-element.4.unit_in, f32[8,256]{1,0:T(8,128)S(1)} %get-tuple-element.5.time_in), custom_call_target="tpu_custom_call" | custom-call | tf_op jit(solution)/shard_map/pallas_call | solution.py:546
